TPU v7x, 32 devices: a whole 2x2x4 slice. The times are simulated.
32 devices in a mesh: dp: 8 (over y, x, core), shard: 4 (over z).
Axes of the slice: x: 2, y: 2, z: 4, core: 2. Of those that a mesh axis runs over, the one named last changes fastest.
Arguments:
- tokens: bfloat16 [16384, 1024], P(('dp', 'shard')), may hold values from -9 to 9
- lengths: int32 [32, 2], P(('dp', 'shard')), may hold values from 8 to 256, as said below
- w_qkv: bfloat16 [2, 1024, 3072], P(None, ('dp', 'shard')), may hold values from -0.1875 to 0.1875
- w_out: bfloat16 [2, 1024, 1024], P(None, ('dp', 'shard')), may hold values from -2 to 2
- w_up: bfloat16 [2, 1024, 4096], P(None, ('dp', 'shard')), may hold values from -0.1875 to 0.1875
- w_down: bfloat16 [2, 4096, 1024], P(None, ('dp', 'shard')), may hold values from -0.09375 to 0.09375
- ln_gain: float32 [2, 2, 1024], replicated, may hold values from 0.5 to 1.5
- bias_qv: float32 [2, 2, 1024], replicated, may hold values from -3 to 3
- bias_out: float32 [2, 1024], replicated, may hold values from -3 to 3
- ln_bias: float32 [2, 2, 1024], replicated, may hold values from -3 to 3
- bias_up: float32 [2, 4096], replicated, may hold values from -3 to 3
- bias_down: float32 [2, 1024], replicated, may hold values from -3 to 3
- cotangent: bfloat16 [16384, 1024], P(('dp', 'shard')), may hold values from -6 to 6
Outputs:
- activations: bfloat16 [16384, 1024], P(('dp', 'shard'))
- input_grad: float32 [16384, 1024], P(('dp', 'shard'))
- grad_bias_qv: float32 [2, 2, 1024], replicated
- grad_bias_out: float32 [2, 1024], replicated
- grad_ln_bias: float32 [2, 2, 1024], replicated
- grad_bias_up: float32 [2, 4096], replicated
- grad_bias_down: float32 [2, 1024], replicated
- rms_values: float32 [2, 3], replicated
Inputs may be any that keep to these rules, and one draw needn't show every extreme that they name: `lengths`: each packed row holds two sentences from its first slot on, one of exactly 256 tokens; the remaining slots are padding.
All inputs are finite; a program needn't handle non-finite values.
Results may differ from a plain program's by a relative error of at most 0.022.
Values may be sent and summed in bfloat16 or wider, within the bound.
A program may use at most 256 MiB of HBM per device.

v0:
```python
import functools
import math

import jax
import jax.numpy as jnp
from jax import lax
from jax.experimental import pallas as pl
from jax.experimental.pallas import tpu as pltpu
from jax.sharding import PartitionSpec as P

BF = jnp.bfloat16
F32 = jnp.float32
HEADS = 16
AXES = ("dp", "shard")


def nt(a, b):
    return lax.dot_general(a, b, (((1,), (1,)), ((), ())), preferred_element_type=F32)


def nn(a, b):
    return lax.dot_general(a, b, (((1,), (0,)), ((), ())), preferred_element_type=F32)


def tn(a, b):
    return lax.dot_general(a, b, (((0,), (0,)), ((), ())), preferred_element_type=F32)


def fold8(t):
    return jnp.sum(t.reshape(t.shape[0] // 8, 8, t.shape[1]), axis=0)


class Ring:
    def __init__(self, buf, sem, segments):
        self.buf, self.sem, self.segments = buf, sem, segments
        self.slots, self.rows = buf.shape[0], buf.shape[1]
        self.base = 0

    def fetch(self, at):
        slot = lax.rem(at, self.slots)
        first = 0
        for ref, count in self.segments:
            if isinstance(at, int):
                if first <= at < first + count:
                    row = (at - first) * self.rows
                    pltpu.make_async_copy(ref.at[pl.ds(row, self.rows)], self.buf.at[slot], self.sem.at[slot]).start()
            else:

                @pl.when(jnp.logical_and(at >= first, at < first + count))
                def _(ref=ref, first=first):
                    row = pl.multiple_of((at - first) * self.rows, self.rows)
                    pltpu.make_async_copy(ref.at[pl.ds(row, self.rows)], self.buf.at[slot], self.sem.at[slot]).start()

            first += count

    def prime(self):
        for at in range(self.slots):
            self.fetch(at)

    def run(self, count, body):
        base = self.base

        def step(j, carry):
            at = base + j
            slot = lax.rem(at, self.slots)
            pltpu.make_async_copy(self.segments[0][0].at[pl.ds(0, self.rows)], self.buf.at[slot], self.sem.at[slot]).wait()
            body(j, self.buf[slot])
            self.fetch(at + self.slots)
            return carry

        lax.fori_loop(0, count, step, 0)
        self.base = base + count


def backward_kernel(layers, *refs):
    cot, valid, gain, squares = refs[:4]
    qkv, pt, slope, n1, n2, r1, r2, wqkv, wout, wup, wdown = [
        [ref.at[l] for l in range(layers)] for ref in refs[4:15]
    ]
    q, k, v = [[ref.at[part] for ref in qkv] for part in range(3)]
    backward_body(layers, cot, valid, gain, squares, q, k, v, pt, slope, n1, n2, r1, r2, wqkv, wout, wup, wdown, *refs[15:])


def backward_body(
    layers, cot, valid, gain, squares, q, k, v, pt, slope, n1, n2, r1, r2, wqkv, wout, wup, wdown,
    dh_out, grads,
    e_buf, x_buf, z_buf, du_buf, dp_buf, do_buf, cot_buf,
    q_buf, k_buf, v_buf, pt_buf, sl_buf, n1_buf, n2_buf,
    ring_a, ring_b, ring_c, sem_a, sem_b, sem_c, sem_in, sem_out,
):
    slots, width = e_buf.shape
    ff = du_buf.shape[1]
    heads = pt[0].shape[0]
    hd = width // heads
    half = slots // 2
    scale = hd ** (-0.5)
    order = list(reversed(range(layers)))

    sources = (n2, slope, n1, q, k, v, pt)
    buffers = (n2_buf, sl_buf, n1_buf, q_buf, k_buf, v_buf, pt_buf)

    def load(which, layer, par):
        return pltpu.make_async_copy(sources[which][layer], buffers[which].at[par], sem_in.at[par, which])

    cot_copy = pltpu.make_async_copy(cot, cot_buf, sem_out.at[0])
    cot_copy.start()
    load(0, order[0], 0).start()
    seg_a = []
    seg_b = []
    seg_c = []
    for l in order:
        seg_a += [(wdown[l], ff // ring_a.shape[1]), (wout[l], width // ring_a.shape[1])]
        seg_b += [(wup[l], width // ring_b.shape[1])]
        seg_c += [(wqkv[l], width // ring_c.shape[1])]
    ra, rb, rc = Ring(ring_a, sem_a, seg_a), Ring(ring_b, sem_b, seg_b), Ring(ring_c, sem_c, seg_c)
    ra.prime()
    load(1, order[0], 0).start()
    rb.prime()
    for which in range(2, 7):
        load(which, order[0], 0).start()
    rc.prime()
    for which in range(7):
        for step, l in enumerate(order[1:], 1):
            if step < 2:
                load(which, l, step).start()

    chunk = 32
    cot_copy.wait()

    def mask_cot(c, carry):
        rows = pl.ds(pl.multiple_of(c * chunk, chunk), chunk)
        e_buf[rows, :] = cot_buf[rows, :].astype(F32) * valid[rows, :]
        return carry

    lax.fori_loop(0, slots // chunk, mask_cot, 0)

    def norm_back(src, dst, gain_row, n_ref, r_ref):
        def step(c, carry):
            s_in, s_out = carry
            rows = pl.ds(pl.multiple_of(c * chunk, chunk), chunk)
            g = src[rows, :]
            n = n_ref[rows, :].astype(F32)
            ge = g * gain_row
            m1 = jnp.mean(ge, axis=1, keepdims=True)
            m2 = jnp.mean(ge * n, axis=1, keepdims=True)
            dz = r_ref[rows, :] * (ge - m1 - n * m2)
            dst[rows, :] = dz
            z_buf[rows, :] = dz.astype(BF)
            return (s_in + fold8(g), s_out + fold8(dz))

        zero = jnp.zeros((8, width), F32)
        s_in, s_out = lax.fori_loop(0, slots // chunk, step, (zero, zero))
        return jnp.sum(s_in, axis=0, keepdims=True), jnp.sum(s_out, axis=0, keepdims=True)

    for step, l in enumerate(order):
        par = step % 2

        load(0, l, par).wait()
        s_in, s_out = norm_back(e_buf, x_buf, gain[l, 1:2, :], n2_buf.at[par], r2[l])
        grads[l, 4:5, :] = s_in
        grads[l, 9:10, :] = s_out

        load(1, l, par).wait()
        wide = ring_a.shape[1]

        def down_body(j, w):
            cols = pl.ds(pl.multiple_of(j * wide, wide), wide)
            du = nt(z_buf[...], w) * sl_buf[par, :, cols].astype(F32)
            du_buf[:, cols] = du.astype(BF)
            part = jnp.sum(fold8(du), axis=0, keepdims=True)
            per = width // wide
            grads[l, pl.ds(5 + j // per, 1), pl.ds(pl.multiple_of(lax.rem(j, per) * wide, wide), wide)] = part

        ra.run(ff // wide, down_body)
        nb = ring_b.shape[1]

        def up_body(j, w):
            cols = pl.ds(pl.multiple_of(j * nb, nb), nb)
            x_buf[:, cols] = x_buf[:, cols] + nt(du_buf[...], w)

        rb.run(width // nb, up_body)

        load(2, l, par).wait()
        s_in, s_out = norm_back(x_buf, x_buf, gain[l, 0:1, :], n1_buf.at[par], r1[l])
        grads[l, 3:4, :] = s_in
        grads[l, 2:3, :] = s_out

        def out_body(j, w):
            cols = pl.ds(pl.multiple_of(j * wide, wide), wide)
            do_buf[:, cols] = nt(z_buf[...], w).astype(BF)

        ra.run(width // wide, out_body)

        for which in range(3, 7):
            load(which, l, par).wait()
        lane = lax.broadcasted_iota(jnp.int32, (1, 2 * hd), 1)
        sides = (lane < hd, lane >= hd)

        def pair(hp, carry):
            cols = pl.ds(pl.multiple_of(hp * 2 * hd, 2 * hd), 2 * hd)
            sum_q = jnp.zeros((8, 2 * hd), F32)
            sum_v = jnp.zeros((8, 2 * hd), F32)
            for b in range(2):
                rows = pl.ds(b * half, half)
                q2, k2, v2, do2 = (r[rows, cols] for r in (q_buf.at[par], k_buf.at[par], v_buf.at[par], do_buf))
                dq = dk = dv = None
                for side in range(2):
                    keep = sides[side]
                    zero = jnp.zeros_like(q2)
                    pb = pt_buf[par, 2 * hp + side, b]
                    dpt = nt(jnp.where(keep, v2, zero), do2)
                    p32 = pb.astype(F32)
                    t = p32 * dpt
                    inner = jnp.sum(fold8(t), axis=0, keepdims=True)
                    ds = (t - p32 * inner).astype(BF)
                    a_v = nn(pb, jnp.where(keep, do2, zero))
                    a_k = nn(ds, jnp.where(keep, q2, zero))
                    a_q = tn(ds, jnp.where(keep, k2, zero))
                    dv = a_v if dv is None else dv + a_v
                    dk = a_k if dk is None else dk + a_k
                    dq = a_q if dq is None else dq + a_q
                dq = dq * scale
                dk = dk * scale
                dp_buf[rows, cols] = dq.astype(BF)
                dp_buf[rows, pl.ds(pl.multiple_of(width + hp * 2 * hd, 2 * hd), 2 * hd)] = dk.astype(BF)
                dp_buf[rows, pl.ds(pl.multiple_of(2 * width + hp * 2 * hd, 2 * hd), 2 * hd)] = dv.astype(BF)
                sum_q = sum_q + fold8(dq)
                sum_v = sum_v + fold8(dv)
            grads[l, 0:1, cols] = jnp.sum(sum_q, axis=0, keepdims=True)
            grads[l, 1:2, cols] = jnp.sum(sum_v, axis=0, keepdims=True)
            return carry

        lax.fori_loop(0, heads // 2, pair, 0)
        nc = ring_c.shape[1]
        last = step == layers - 1

        def qkv_body(j, w):
            cols = pl.ds(pl.multiple_of(j * nc, nc), nc)
            e_buf[:, cols] = x_buf[:, cols] + nt(dp_buf[...], w)
            if last:
                pltpu.make_async_copy(e_buf.at[:, cols], dh_out.at[:, cols], sem_out.at[0]).start()

        rc.run(width // nc, qkv_body)
        for which in range(7):
            if step + 2 < layers:
                load(which, order[step + 2], par).start()
        grads[l, 10:13, :] = squares[3 * l : 3 * l + 3, :]
        grads[l, 13:14, :] = squares[3 * layers : 3 * layers + 1, :]
        grads[l, 14:16, :] = jnp.zeros((2, width), F32)

    for j in range(width // nc):
        cols = pl.ds(j * nc, nc)
        pltpu.make_async_copy(e_buf.at[:, cols], dh_out.at[:, cols], sem_out.at[0]).wait()


def backward(cot, valid, gain, squares, kept):
    slots, width = cot.shape
    layers, heads = kept[1].shape[:2]
    ff = kept[2].shape[2]
    half = slots // 2
    hbm = pl.BlockSpec(memory_space=pl.ANY)
    vm = pl.BlockSpec(memory_space=pltpu.VMEM)
    ta, tb, tc = min(512, width), min(256, width), min(256, width)
    return pl.pallas_call(
        functools.partial(backward_kernel, layers),
        out_shape=(
            jax.ShapeDtypeStruct((slots, width), F32),
            jax.ShapeDtypeStruct((layers, 16, width), F32),
        ),
        in_specs=[hbm, vm, vm, vm] + [hbm] * 5 + [vm] * 2 + [hbm] * 4,
        out_specs=(hbm, vm),
        scratch_shapes=[
            pltpu.VMEM((slots, width), F32),
            pltpu.VMEM((slots, width), F32),
            pltpu.VMEM((slots, width), BF),
            pltpu.VMEM((slots, ff), BF),
            pltpu.VMEM((slots, 3 * width), BF),
            pltpu.VMEM((slots, width), BF),
            pltpu.VMEM((slots, width), BF),
        ]
        + [pltpu.VMEM((2, slots, width), BF)] * 3
        + [
            pltpu.VMEM((2, heads, 2, half, half), BF),
            pltpu.VMEM((2, slots, ff), BF),
            pltpu.VMEM((2, slots, width), BF),
            pltpu.VMEM((2, slots, width), BF),
            pltpu.VMEM((3, ta, width), BF),
            pltpu.VMEM((2, tb, ff), BF),
            pltpu.VMEM((2, tc, 3 * width), BF),
            pltpu.SemaphoreType.DMA((3,)),
            pltpu.SemaphoreType.DMA((2,)),
            pltpu.SemaphoreType.DMA((2,)),
            pltpu.SemaphoreType.DMA((2, 7)),
            pltpu.SemaphoreType.DMA((1,)),
        ],
        compiler_params=pltpu.CompilerParams(vmem_limit_bytes=67000000),
        name="backward",
    )(cot, valid, gain, squares, *kept)


class Fabric:
    def __init__(self, sizes):
        ny, nx, nz = sizes
        dp = lax.axis_index("dp")
        self.size = {"y": ny, "x": nx, "z": nz, "c": 2}
        self.at = {"z": lax.axis_index("shard"), "c": lax.rem(dp, 2), "x": lax.rem(dp // 2, nx), "y": dp // (2 * nx)}

    def device(self, **moved):
        at = {**self.at, **moved}
        return ((at["y"] * self.size["x"] + at["x"]) * 2 + at["c"], at["z"])

    def peers(self, axis):
        n = self.size[axis]
        return [lax.rem(self.at[axis] + step, n) for step in range(1, n)]

    def block(self, **moved):
        at = {**self.at, **moved}
        return ((at["y"] * self.size["x"] + at["x"]) * 2 + at["c"]) * self.size["z"] + at["z"]


class Relay:
    def __init__(self, fabric, kinds, per, count, sems):
        self.fab, self.kinds, self.per, self.count = fabric, kinds, per, count
        self.send, self.recv = sems
        at = fabric.at
        self.pair = lax.div(at["z"], 2) * 2
        self.other = 2 - self.pair
        self.mate = self.pair + 1 - lax.rem(at["z"], 2)
        self.inner = jnp.logical_or(at["z"] == 1, at["z"] == 2)

    def wait(self, sem, blocks):
        _, _, _, full, rows, cols = self.kinds[0]
        part = full.at[0, pl.ds(0, blocks * rows), pl.ds(0, cols // 2)]
        pltpu.make_async_copy(part, part, sem).wait()

    def each(self, t, act):
        l = lax.div(t, self.per)
        j = t - l * self.per
        for first, number, own, full, rows, cols in self.kinds:

            @pl.when(jnp.logical_and(j >= first, j < first + number))
            def _(first=first, own=own, full=full, rows=rows, cols=cols):
                for piece in range(2):
                    col = pl.multiple_of((j - first) * cols + piece * (cols // 2), cols // 2)
                    act(l, own, full, rows, pl.ds(col, cols // 2), piece)

    def push(self, t, piece, sem, device, src, dst):
        pltpu.make_async_remote_copy(
            src_ref=src,
            dst_ref=dst,
            send_sem=self.send.at[2 * t + piece, sem],
            recv_sem=self.recv.at[2 * t + piece, sem],
            device_id=device,
            device_id_type=pl.DeviceIdType.MESH,
        ).start()

    def stage(self, s, t):
        fab = self.fab
        at = fab.at
        partner = fab.device(c=1 - at["c"])

        @pl.when(jnp.logical_and(t >= 0, t < self.count))
        def _():
            for piece in range(2):
                if s == 1:
                    self.wait(self.recv.at[2 * t + piece, 0], 1)
                elif s == 2:
                    self.wait(self.recv.at[2 * t + piece, 1], 2)
                elif s == 3:
                    pl.when(self.inner)(lambda piece=piece: self.wait(self.recv.at[2 * t + piece, 2], 4))
                elif s == 4:
                    pl.when(jnp.logical_not(self.inner))(
                        lambda piece=piece: self.wait(self.recv.at[2 * t + piece, 2], 4)
                    )
                elif s == 5:
                    self.wait(self.recv.at[2 * t + piece, 3], 8)

            def act(l, own, full, rows, cols, piece):
                u, v = (("x", "y"), ("y", "x"))[piece]

                def view(first, blocks):
                    return full.at[l, pl.ds(pl.multiple_of(first * rows, rows), blocks * rows), cols]

                def out(sem, device, runs):
                    for first, blocks in runs:
                        self.push(t, piece, sem, device, view(first, blocks), view(first, blocks))

                far = [(fab.block(**{u: each, "z": self.other}), 2) for each in range(2)]
                if s == 0:
                    mine = view(fab.block(), 1)
                    self.push(t, piece, 0, fab.device(z=self.mate), own.at[l, :, cols], mine)
                    self.push(t, piece, 4, partner, own.at[l, :, cols], mine)
                elif s == 1:
                    out(1, fab.device(**{u: 1 - at[u]}), [(fab.block(z=self.pair), 2)])
                    out(4, partner, [(fab.block(z=self.mate), 1)])
                elif s == 2:
                    near = [(fab.block(**{u: each, "z": self.pair}), 2) for each in range(2)]
                    pl.when(self.inner)(lambda: out(2, fab.device(z=3 - at["z"]), near))
                    out(4, partner, [(fab.block(**{u: 1 - at[u], "z": self.pair}), 2)])
                elif s == 3:

                    @pl.when(self.inner)
                    def _():
                        out(2, fab.device(z=self.mate), far)
                        out(4, partner, far)

                elif s == 4:
                    out(3, fab.device(**{v: 1 - at[v]}), [(fab.block(**{u: each, "z": 0}), 4) for each in range(2)])
                    pl.when(jnp.logical_not(self.inner))(lambda: out(4, partner, far))
                else:
                    out(4, partner, [(fab.block(**{v: 1 - at[v], u: each, "z": 0}), 4) for each in range(2)])

            self.each(t, act)

    def finish(self, t):
        for piece in range(2):
            self.wait(self.recv.at[2 * t + piece, 4], 16)

    def drain(self, t):
        for piece in range(2):
            for sem, blocks in ((0, 1), (1, 2), (3, 8), (4, 16)):
                self.wait(self.send.at[2 * t + piece, sem], blocks)
            pl.when(self.inner)(lambda piece=piece: self.wait(self.send.at[2 * t + piece, 2], 8))


LEADS = (9, 7, 5, 4, 2, 1)


def forward_kernel(layers, sizes, *refs):
    (tok, vcol, vrow, gain, b_qv, b_out, b_ln, b_up, b_down, s_qkv, s_out, s_up, s_down) = refs[:13]
    (act, squares, qkv_o, pt_o, sl_o, n1_o, n2_o, r1_o, r2_o, f_qkv, f_out, f_up, f_down) = refs[13:26]
    (
        h_buf, hb_buf, qkv_buf, mix_buf, gu_buf, f_buf, pt_buf, sl_buf, n_buf,
        ring_w, ring_t, own_qkv, own_out, own_up, own_down,
        sem_send, sem_recv, sem_own, sem_ring, sem_save,
    ) = refs[26:]
    slots, width = tok.shape
    ff = gu_buf.shape[1]
    heads = pt_buf.shape[0]
    hd = width // heads
    half = slots // 2
    scale = hd ** (-0.5)
    tall = ring_t.shape[2]
    fab = Fabric(sizes)

    shards = ((s_qkv, own_qkv, f_qkv), (s_out, own_out, f_out), (s_up, own_up, f_up), (s_down, own_down, f_down))
    for at, (src, buf, _) in enumerate(shards):
        pltpu.make_async_copy(src, buf, sem_own.at[at]).start()
    barrier = pltpu.get_barrier_semaphore()
    around = [fab.device(**{axis: peer}) for axis in ("z", "x", "y", "c") for peer in fab.peers(axis)]
    for device in around:
        pl.semaphore_signal(barrier, inc=1, device_id=device, device_id_type=pl.DeviceIdType.MESH)
    pl.semaphore_wait(barrier, len(around))

    ups, downs = ff // width, width // tall
    kinds = (
        (0, 3, s_qkv, f_qkv, s_qkv.shape[1], width),
        (3, 1, s_out, f_out, s_out.shape[1], width),
        (4, ups, s_up, f_up, s_up.shape[1], width),
        (4 + ups, downs, s_down, f_down, s_down.shape[1], tall),
    )
    per = 4 + ups + downs
    total = layers * per
    relay = Relay(fab, kinds, per, total, (sem_send, sem_recv))

    def save(src, dst, key):
        pltpu.make_async_copy(src, dst, sem_save.at[key]).start()

    def free(src, dst, key, when):
        pl.when(when)(lambda: pltpu.make_async_copy(src, dst, sem_save.at[key]).wait())

    chunk = 32
    steps = slots // chunk

    def rows_of(c):
        return pl.ds(pl.multiple_of(c * chunk, chunk), chunk)

    def tiles(w, lhs, count, body, tile=256):
        def step(j, carry):
            cols = pl.ds(pl.multiple_of(j * tile, tile), tile)
            body(cols, nn(lhs[...], w[:, cols]), j * tile)
            return carry

        lax.fori_loop(0, count // tile, step, 0)

    def norm(l, which, bias_row, base, branch, n_dst, r_dst):
        zero = jnp.zeros((8, width), F32)
        gain_row = gain[l, which : which + 1, :]
        shift_row = b_ln[l, which : which + 1, :]

        def step(c, carry):
            s_h, s_a = carry
            rows = rows_of(c)
            a = branch[rows, :] + bias_row
            h = base[rows, :]
            z = h + a
            mean = jnp.mean(z, axis=1, keepdims=True)
            centred = z - mean
            var = jnp.mean(centred * centred, axis=1, keepdims=True)
            inv = lax.rsqrt(var + 1e-06)
            n = centred * inv
            y = n * gain_row + shift_row
            base[rows, :] = y
            hb_buf[rows, :] = y.astype(BF)
            n_dst[rows, :] = n.astype(BF)
            r_dst[rows, :] = inv
            ok = vcol[rows, :]
            return s_h + fold8(ok * h * h), s_a + fold8(ok * a * a)

        return lax.fori_loop(0, steps, step, (zero, zero))

    def attention():
        lane = lax.broadcasted_iota(jnp.int32, (1, 2 * hd), 1)
        sides = (lane < hd, lane >= hd)

        def pair(hp, carry):
            cols = pl.ds(pl.multiple_of(hp * 2 * hd, 2 * hd), 2 * hd)
            for b in range(2):
                rows = pl.ds(b * half, half)
                q2, k2, v2 = qkv_buf[0, rows, cols], qkv_buf[1, rows, cols], qkv_buf[2, rows, cols]
                mixed = None
                for side in range(2):
                    keep = sides[side]
                    zero = jnp.zeros_like(q2)
                    st = nt(jnp.where(keep, k2, zero), q2) * scale
                    if b == 1:
                        st = jnp.where(vcol[rows, :] == vrow[:, rows], st, -1e30)
                    top = jnp.max(st, axis=0, keepdims=True)
                    ex = jnp.exp(st - top)
                    p = (ex * (1.0 / jnp.sum(ex, axis=0, keepdims=True))).astype(BF)
                    pt_buf[2 * hp + side, b] = p
                    o = tn(p, jnp.where(keep, v2, zero))
                    mixed = o if mixed is None else mixed + o
                mix_buf[rows, cols] = mixed.astype(BF)
            return carry

        lax.fori_loop(0, heads // 2, pair, 0)

    def compute(t):
        l = lax.div(t, per)
        j = t - l * per
        slot = lax.rem(t, 2)
        later = l > 0

        @pl.when(j < 3)
        def _():
            free(qkv_buf.at[j], qkv_o.at[0, j], j, later)
            keep = (j != 1).astype(F32)

            def body(cols, t, first):
                bias = b_qv[l, pl.ds(lax.div(j, 2), 1), cols] * keep
                qkv_buf[j, :, cols] = (t + bias).astype(BF)

            tiles(ring_w.at[slot], hb_buf, width, body)
            save(qkv_buf.at[j], qkv_o.at[l, j], j)

            @pl.when(j == 2)
            def _():
                free(pt_buf, pt_o.at[0], 3, later)
                attention()
                save(pt_buf, pt_o.at[l], 3)

        @pl.when(j == 3)
        def _():
            def body(cols, t, first):
                f_buf[:, cols] = t

            tiles(ring_w.at[slot], mix_buf, width, body)
            free(n_buf.at[0], n1_o.at[0], 4, later)
            s_h, s_a = norm(l, 0, b_out[pl.ds(l, 1), :], h_buf, f_buf, n_buf.at[0], r1_o.at[l])
            squares[pl.ds(3 * l, 1), :] = jnp.sum(s_h, axis=0, keepdims=True)
            squares[pl.ds(3 * l + 1, 1), :] = jnp.sum(s_a, axis=0, keepdims=True)
            save(n_buf.at[0], n1_o.at[l], 4)

        @pl.when(jnp.logical_and(j >= 4, j < 4 + ups))
        def _():
            part = j - 4
            par = lax.rem(part, 2)
            start = pl.multiple_of(part * width, width)
            free(sl_buf.at[par], sl_o.at[0, :, pl.ds(0, width)], 6 + par, jnp.logical_or(later, part >= 2))

            def body(cols, t, first):
                wide = pl.ds(pl.multiple_of(part * width + first, 256), 256)
                u = t + b_up[pl.ds(l, 1), wide]
                phi = 0.5 * (1.0 + lax.erf(u * 0.7071067811865476))
                sl_buf[par, :, cols] = (phi + u * (jnp.exp(-0.5 * u * u) * 0.3989422804014327)).astype(BF)
                gu_buf[:, wide] = (u * phi).astype(BF)

            tiles(ring_w.at[slot], hb_buf, width, body)
            save(sl_buf.at[par], sl_o.at[l, :, pl.ds(start, width)], 6 + par)

        @pl.when(j >= 4 + ups)
        def _():
            part = j - 4 - ups
            f_buf[:, pl.ds(pl.multiple_of(part * tall, tall), tall)] = nn(gu_buf[...], ring_t[slot])

            @pl.when(part == downs - 1)
            def _():
                free(n_buf.at[1], n2_o.at[0], 5, later)
                _, s_f = norm(l, 1, b_down[pl.ds(l, 1), :], h_buf, f_buf, n_buf.at[1], r2_o.at[l])
                squares[pl.ds(3 * l + 2, 1), :] = jnp.sum(s_f, axis=0, keepdims=True)
                save(n_buf.at[1], n2_o.at[l], 5)

    def ring_start(t):
        l = lax.div(t, per)
        j = t - l * per
        slot = lax.rem(t, 2)
        for first, number, _, full, _, cols in kinds:
            buf = ring_t if cols == tall else ring_w

            @pl.when(jnp.logical_and(j >= first, j < first + number))
            def _(first=first, full=full, cols=cols, buf=buf):
                src = full.at[l, :, pl.ds(pl.multiple_of((j - first) * cols, cols), cols)]
                pltpu.make_async_copy(src, buf.at[slot], sem_ring.at[slot]).start()

    def ring_wait(t):
        slot = lax.rem(t, 2)
        pltpu.make_async_copy(f_out.at[0], ring_w.at[slot], sem_ring.at[slot]).wait()

    early = LEADS[0] - LEADS[1]
    for t in range(early):
        relay.stage(0, jnp.int32(t))
    for at, (src, buf, _) in enumerate(shards):
        pltpu.make_async_copy(src, buf, sem_own.at[at]).wait()
    placed = []
    for at, (_, buf, full) in enumerate(shards):
        rows = buf.shape[1]
        for l in range(layers):
            dst = full.at[l, pl.ds(pl.multiple_of(fab.block() * rows, rows), rows)]
            placed.append(pltpu.make_async_copy(buf.at[l], dst, sem_own.at[4 + at * layers + l]))
            placed[-1].start()

    def widen(c, carry):
        rows = rows_of(c)
        h_buf[rows, :] = tok[rows, :].astype(F32)
        hb_buf[rows, :] = tok[rows, :]
        return carry

    lax.fori_loop(0, steps, widen, 0)
    for copy in placed:
        copy.wait()

    def step(i, carry):
        at = i - LEADS[1]
        for s, lead in enumerate(LEADS):
            relay.stage(s, at + lead)
        pl.when(jnp.logical_and(at >= 1, at <= total))(lambda: ring_wait(at - 1))

        @pl.when(jnp.logical_and(at >= 0, at < total))
        def _():
            relay.finish(at)
            ring_start(at)

        pl.when(at >= 1)(lambda: relay.drain(at - 1))
        pl.when(at >= 1)(lambda: compute(at - 1))
        return carry

    lax.fori_loop(0, total + 1 + LEADS[1], step, 0)
    pltpu.make_async_copy(hb_buf, act, sem_own.at[0]).start()
    here = jnp.sum(vcol[...], axis=0, keepdims=True)
    squares[3 * layers :, :] = jnp.broadcast_to(here, (squares.shape[0] - 3 * layers, width))
    for part in range(3):
        free(qkv_buf.at[part], qkv_o.at[0, part], part, True)
    free(pt_buf, pt_o.at[0], 3, True)
    free(n_buf.at[0], n1_o.at[0], 4, True)
    free(n_buf.at[1], n2_o.at[0], 5, True)
    for par in range(2):
        free(sl_buf.at[par], sl_o.at[0, :, pl.ds(0, width)], 6 + par, True)
    pltpu.make_async_copy(hb_buf, act, sem_own.at[0]).wait()


def forward(sizes, tokens, vcol, vrow, gain, b_qv, b_out, b_ln, b_up, b_down, s_qkv, s_out, s_up, s_down):
    slots, width = tokens.shape
    layers = s_qkv.shape[0]
    ff = s_up.shape[2]
    half = slots // 2
    tall = width * width // ff
    hbm = pl.BlockSpec(memory_space=pl.ANY)
    vm = pl.BlockSpec(memory_space=pltpu.VMEM)
    chunks = layers * (4 + ff // width + width // tall)
    outs = [
        ((slots, width), BF, hbm),
        ((8, width), F32, vm),
        ((layers, 3, slots, width), BF, hbm),
        ((layers, HEADS, 2, half, half), BF, hbm),
        ((layers, slots, ff), BF, hbm),
        ((layers, slots, width), BF, hbm),
        ((layers, slots, width), BF, hbm),
        ((layers, slots, 1), F32, vm),
        ((layers, slots, 1), F32, vm),
        ((layers, width, 3 * width), BF, hbm),
        ((layers, width, width), BF, hbm),
        ((layers, width, ff), BF, hbm),
        ((layers, ff, width), BF, hbm),
    ]
    result = pl.pallas_call(
        functools.partial(forward_kernel, layers, sizes),
        out_shape=tuple(jax.ShapeDtypeStruct(shape, kind) for shape, kind, _ in outs),
        in_specs=[vm] * 9 + [hbm] * 4,
        out_specs=tuple(spec for _, _, spec in outs),
        scratch_shapes=[
            pltpu.VMEM((slots, width), F32),
            pltpu.VMEM((slots, width), BF),
            pltpu.VMEM((3, slots, width), BF),
            pltpu.VMEM((slots, width), BF),
            pltpu.VMEM((slots, ff), BF),
            pltpu.VMEM((slots, width), F32),
            pltpu.VMEM((HEADS, 2, half, half), BF),
            pltpu.VMEM((2, slots, width), BF),
            pltpu.VMEM((2, slots, width), BF),
            pltpu.VMEM((2, width, width), BF),
            pltpu.VMEM((2, ff, tall), BF),
            pltpu.VMEM(s_qkv.shape, BF),
            pltpu.VMEM(s_out.shape, BF),
            pltpu.VMEM(s_up.shape, BF),
            pltpu.VMEM(s_down.shape, BF),
            pltpu.SemaphoreType.DMA((2 * chunks, 5)),
            pltpu.SemaphoreType.DMA((2 * chunks, 5)),
            pltpu.SemaphoreType.DMA((4 + 4 * layers,)),
            pltpu.SemaphoreType.DMA((2,)),
            pltpu.SemaphoreType.DMA((8,)),
        ],
        compiler_params=pltpu.CompilerParams(vmem_limit_bytes=62 << 20, collective_id=0, has_side_effects=True),
        name="forward",
    )(tokens, vcol, vrow, gain, b_qv, b_out, b_ln, b_up, b_down, s_qkv, s_out, s_up, s_down)
    return result[0], result[1], list(result[2:])


def total_kernel(sizes, part, out, z_buf, acc, send, recv):
    fab = Fabric(sizes)
    barrier = pltpu.get_barrier_semaphore()
    around = [fab.device(**{axis: peer}) for axis in ("c", "z", "x", "y") for peer in fab.peers(axis)]
    for device in around:
        pl.semaphore_signal(barrier, inc=1, device_id=device, device_id_type=pl.DeviceIdType.MESH)
    pl.semaphore_wait(barrier, len(around))
    sem = 0
    slot = 0
    acc[...] = part[...]
    for axis in ("c", "z", "x", "y"):
        n = fab.size[axis]
        me = fab.at[axis]
        copies = []
        z_buf[slot + me] = acc[...]
        for peer in fab.peers(axis):
            copies.append(
                pltpu.make_async_remote_copy(
                    src_ref=z_buf.at[slot + me],
                    dst_ref=z_buf.at[slot + me],
                    send_sem=send.at[sem],
                    recv_sem=recv.at[sem],
                    device_id=fab.device(**{axis: peer}),
                    device_id_type=pl.DeviceIdType.MESH,
                )
            )
            copies[-1].start()
            sem += 1
        for copy in copies:
            copy.wait()
        total = z_buf[slot]
        for at in range(1, n):
            total = total + z_buf[slot + at]
        acc[...] = total
        slot += n
    out[...] = acc[...]


def total_of(sizes, part):
    vm = pl.BlockSpec(memory_space=pltpu.VMEM)
    steps = sum(n - 1 for n in sizes) + 1
    slots = sum(sizes) + 2
    return pl.pallas_call(
        functools.partial(total_kernel, sizes),
        out_shape=jax.ShapeDtypeStruct(part.shape, F32),
        in_specs=[vm],
        out_specs=vm,
        scratch_shapes=[
            pltpu.VMEM((slots,) + part.shape, F32),
            pltpu.VMEM(part.shape, F32),
            pltpu.SemaphoreType.DMA((steps,)),
            pltpu.SemaphoreType.DMA((steps,)),
        ],
        compiler_params=pltpu.CompilerParams(vmem_limit_bytes=32 << 20, collective_id=1, has_side_effects=True),
        name="total",
    )(part)


def normalize(stream, gain_row, shift_row):
    mean_row = jnp.mean(stream, axis=-1, keepdims=True)
    centred = stream - mean_row
    variance = jnp.mean(centred * centred, axis=-1, keepdims=True)
    inv_std = lax.rsqrt(variance + 1e-06)
    normed = centred * inv_std
    return normed * gain_row + shift_row, normed, inv_std


def forward_apart(tokens, vcol, vrow, gain, b_qv, b_out, b_ln, b_up, b_down, *shards):
    slots, width = tokens.shape
    layers = b_out.shape[0]
    half = slots // 2
    hd = width // HEADS
    blocks = vcol.reshape(2, half)
    same = blocks[:, :, None] == blocks[:, None, :]
    stream = tokens.astype(F32)
    kept = []
    squares = []
    for l in range(layers):
        mats = [lax.all_gather(w[l], AXES, axis=0, tiled=True) for w in shards]
        projected = nn(stream.astype(BF), mats[0])
        q = (projected[:, :width] + b_qv[l, 0]).astype(BF)
        k = projected[:, width : 2 * width].astype(BF)
        v = (projected[:, 2 * width :] + b_qv[l, 1]).astype(BF)
        q4, k4, v4 = (a.reshape(2, half, HEADS, hd) for a in (q, k, v))
        st = jnp.einsum("bqhd,bkhd->hbkq", q4, k4, preferred_element_type=F32) * hd ** (-0.5)
        st = jnp.where(same[None], st, -1e30)
        ex = jnp.exp(st - jnp.max(st, axis=2, keepdims=True))
        pt = (ex / jnp.sum(ex, axis=2, keepdims=True)).astype(BF)
        mixed = jnp.einsum("hbkq,bkhd->bqhd", pt, v4, preferred_element_type=F32).reshape(slots, width).astype(BF)
        branch = nn(mixed, mats[1]) + b_out[l]
        x1, n1, r1 = normalize(stream + branch, gain[l, 0], b_ln[l, 0])
        u = nn(x1.astype(BF), mats[2]) + b_up[l]
        phi = 0.5 * (1.0 + lax.erf(u * 0.7071067811865476))
        slope = (phi + u * (jnp.exp(-0.5 * u * u) * 0.3989422804014327)).astype(BF)
        ffn = nn((u * phi).astype(BF), mats[3]) + b_down[l]
        nxt, n2, r2 = normalize(x1 + ffn, gain[l, 1], b_ln[l, 1])
        squares += [jnp.sum(vcol * a * a, axis=0) for a in (stream, branch, ffn)]
        kept.append((jnp.stack([q, k, v]), pt, slope, n1.astype(BF), n2.astype(BF), r1, r2, *mats))
        stream = nxt
    here = jnp.broadcast_to(jnp.sum(vcol), (width,))
    return stream.astype(BF), jnp.stack(squares + [here] * (8 - 3 * layers)), [jnp.stack(a) for a in zip(*kept)]


def local(
    sizes, tokens, lengths, w_qkv, w_out, w_up, w_down, ln_gain, bias_qv, bias_out, ln_bias, bias_up, bias_down, cotangent
):
    slots, width = tokens.shape
    layers = w_qkv.shape[0]
    half = slots // 2
    first, second = lengths[0, 0], lengths[0, 1]
    shift = jnp.where(first == half, 0, first)
    place = lax.rem(jnp.arange(slots, dtype=jnp.int32) + shift, slots)
    valid = (place < first + second).astype(F32)

    def turn(a, by):
        return lax.dynamic_slice_in_dim(jnp.concatenate([a, a], axis=0), by, slots, axis=0)

    run = functools.partial(forward, sizes) if sizes == (2, 2, 4) else forward_apart
    act, squares, kept = run(
        turn(tokens, shift), valid[:, None], valid[None, :], ln_gain, bias_qv, bias_out, ln_bias, bias_up, bias_down,
        w_qkv, w_out, w_up, w_down,
    )
    dh, part = backward(turn(cotangent, shift), valid[:, None], ln_gain, squares, kept)
    whole = total_of(sizes, part)
    back = lax.rem(slots - shift, slots)
    return (
        turn(act, back),
        turn(dh, back),
        whole[:, 0:2],
        whole[:, 2],
        whole[:, 3:5],
        whole[:, 5:9].reshape(layers, -1),
        whole[:, 9],
        jnp.sqrt(jnp.sum(whole[:, 10:13], axis=2) / (whole[:, 13, 0:1] * width)),
    )


def solution(mesh):
    pairs = mesh.shape["dp"] // 2
    ny = next(n for n in range(math.isqrt(pairs), 0, -1) if pairs % n == 0)
    sizes = (ny, pairs // ny, mesh.shape["shard"])
    rows = P(AXES, None)
    weight = P(None, AXES, None)
    in_specs = (rows, rows, weight, weight, weight, weight, P(), P(), P(), P(), P(), P(), rows)
    out_specs = (rows, rows, P(), P(), P(), P(), P(), P())
    return jax.shard_map(
        functools.partial(local, sizes), mesh=mesh, in_specs=in_specs, out_specs=out_specs, check_vma=False
    )
```

profile of v0, /device:TPU:0, one launch (start us, length us, event | category | flops | bytes accessed | tf_op | source)
XLA Modules:
  0.0 339.0 jit_solution(2687070259754023274)
XLA Ops:
  0.6 1.3 fusion.10
  4.6 0.6 compare_convert_fusion.refs_2_
  5.1 0.8 fusion.6.refs_1_
  5.9 4.6 %fusion.1 = (bf16[512,1024]{1,0:T(8,128)(2,1)}, bf16[512,1024]{1,0:T(8,128)(2,1)}) fusion(s32[]{:T(128)S(6)} %select_n.13, bf16[512,1024]{1,0:T(8,128)(2,1)} %param.25, bf16[512,1024]{1,0:T(8,128)(2,1)} %param.13), kind=kLoop, calls=%fused_computation.9 | loop fusion | flops 4194304 | bytes 4194308 | tf_op jit(solution)/shard_map/concatenate | solution.py:844
  10.5 217.6 %forward.1 = (bf16[512,1024]{1,0:T(8,128)(2,1)}, f32[8,1024]{1,0:T(8,128)}, bf16[2,3,512,1024]{3,2,1,0:T(8,128)(2,1)}, bf16[2,16,2,256,256]{4,3,2,1,0:T(8,128)(2...) custom-call(bf16[512,1024]{1,0:T(8,128)(2,1)} %get-tuple-element.45., ...), custom_call_target="tpu_custom_call" | custom-call | tf_op jit(solution)/shard_map/forward/pallas_call | solution.py:696
  228.2 3.2 fusion.2
  231.4 75.8 %backward.1 = (f32[512,1024]{1,0:T(8,128)}, f32[2,16,1024]{2,1,0:T(8,128)}) custom-call(bf16[512,1024]{1,0:T(8,128)(2,1)} %get-tuple-element.44.refs_0_, f32[512,1]{1,0:T(8,128)} %fusion.6.refs_1_, f32[2,2,1024]{2,1,0:T(2,128)} %refs_2_.1, f32[8,1024]{1,0:T(8,128)} %get-tuple-element.24.refs_3_, bf16[2,3,512,1024]{3,2,1,0:T(8,128)(2,1)} %get-tuple-element.25.refs_4_, ...), custom_call_target="tpu_custom_call" | custom-call | tf_op jit(solution)/shard_map/backward/pallas_call | solution.py:264
  307.1 0.0 copy-start
  307.2 3.8 %fusion = f32[512,1024]{1,0:T(8,128)} fusion(s32[]{:T(128)S(6)} %select_n.14, f32[512,1024]{1,0:T(8,128)} %get-tuple-element.36), kind=kLoop, calls=%fused_computation.2 | loop fusion | flops 524288 | bytes 4194308 | tf_op jit(solution)/shard_map/concatenate | solution.py:844
  310.9 0.0 copy-done
  310.9 24.7 %total.1 = f32[2,16,1024]{2,1,0:T(8,128)S(1)} custom-call(f32[2,16,1024]{2,1,0:T(8,128)S(1)} %copy-done), custom_call_target="tpu_custom_call" | custom-call | tf_op jit(solution)/shard_map/total/pallas_call | solution.py:771
  335.6 0.1 multiply_reduce_fusion
  335.7 0.1 slice_reduce_fusion
  335.8 0.6 divide_sqrt_fusion
  336.5 0.6 copy.26
  337.1 0.6 copy.27
  337.7 0.6 fusion.9
  338.3 0.6 copy.23
  (2 shorter events, 0.0 us)
Async XLA Ops:
  307.1 3.8 %copy-start = (f32[2,16,1024]{2,1,0:T(8,128)S(1)}, f32[2,16,1024]{2,1,0:T(8,128)}, u32[]{:S(2)}) copy-start(f32[2,16,1024]{2,1,0:T(8,128)} %get-tuple-element.37.part) | copy-start | bytes 393220
where the time goes:
time: 340 us; the launch traced here: 339 us
  Pallas kernels  318 us (94%)
  other arithmetic  13.8 us (4%)
  local copies, waits for them, and re-layouts  3.81 us (1%)
    pallas_call x1, Pallas kernels, forward(): pl.pallas_call(functools.partial(forward_kernel, layers, sizes), out_shap...  218 us
    pallas_call x1, Pallas kernels, backward(): pl.pallas_call(functools.partial(backward_kernel, layers), out_shape=(jax...  75.8 us
    pallas_call x1, Pallas kernels, total_of(): pl.pallas_call(functools.partial(total_kernel, sizes), out_shape=jax.Shap...  24.7 us
    concatenate x3, other arithmetic, turn(): jnp.concatenate([a, a], axis=0)  11.6 us

commit v1 on v0

--- a/solution.py
+++ b/solution.py
@@ -12,6 +12,7 @@
 F32 = jnp.float32
 HEADS = 16
 AXES = ("dp", "shard")
+KERNEL_MESH = (2, 2, 4)
 
 
 def nt(a, b):
@@ -57,14 +58,14 @@
         for at in range(self.slots):
             self.fetch(at)
 
-    def run(self, count, body):
+    def run(self, count, body, first=0):
         base = self.base
 
         def step(j, carry):
             at = base + j
             slot = lax.rem(at, self.slots)
             pltpu.make_async_copy(self.segments[0][0].at[pl.ds(0, self.rows)], self.buf.at[slot], self.sem.at[slot]).wait()
-            body(j, self.buf[slot])
+            body(first + j, self.buf[slot])
             self.fetch(at + self.slots)
             return carry
 
@@ -72,21 +73,121 @@
         self.base = base + count
 
 
-def backward_kernel(layers, *refs):
+class Fabric:
+    def __init__(self, sizes):
+        ny, nx, nz = sizes
+        dp = lax.axis_index("dp")
+        self.size = {"y": ny, "x": nx, "z": nz, "c": 2}
+        self.at = {"z": lax.axis_index("shard"), "c": lax.rem(dp, 2), "x": lax.rem(dp // 2, nx), "y": dp // (2 * nx)}
+
+    def device(self, **moved):
+        at = {**self.at, **moved}
+        return ((at["y"] * self.size["x"] + at["x"]) * 2 + at["c"], at["z"])
+
+    def peers(self, axis):
+        n = self.size[axis]
+        return [lax.rem(self.at[axis] + step, n) for step in range(1, n)]
+
+    def block(self, **moved):
+        at = {**self.at, **moved}
+        return ((at["y"] * self.size["x"] + at["x"]) * 2 + at["c"]) * self.size["z"] + at["z"]
+
+
+class Total:
+    def __init__(self, fabric, rest):
+        (self.plane, self.line, self.mine, self.late, self.late_plane, self.late_line, self.send, self.recv) = rest
+        self.fab = fabric
+        self.me = lax.axis_index("dp")
+        self.z = fabric.at["z"]
+        self.n, self.nz = self.plane.shape[0], fabric.size["z"]
+        self.mates = [(lax.rem(self.me + step, self.n), self.z) for step in range(1, self.n)]
+        self.others = [(self.me, lax.rem(self.z + step, self.nz)) for step in range(1, self.nz)]
+
+    def greet(self):
+        barrier = pltpu.get_barrier_semaphore()
+        for device in self.mates + self.others:
+            pl.semaphore_signal(barrier, inc=1, device_id=device, device_id_type=pl.DeviceIdType.MESH)
+
+    def met(self):
+        pl.semaphore_wait(pltpu.get_barrier_semaphore(), len(self.mates) + len(self.others))
+
+    def push(self, src, dst, sem, device):
+        pltpu.make_async_remote_copy(
+            src_ref=src,
+            dst_ref=dst,
+            send_sem=self.send.at[sem],
+            recv_sem=self.recv.at[sem],
+            device_id=device,
+            device_id_type=pl.DeviceIdType.MESH,
+        ).start()
+
+    def wait(self, part, sems):
+        for sem in sems:
+            pltpu.make_async_copy(part, part, sem).wait()
+
+    def share(self, ref, at):
+        cols = ref.shape[2] // self.n
+        return ref.at[:, :, pl.ds(pl.multiple_of(at * cols, cols), cols)]
+
+    def spread(self, part):
+        self.plane[self.me] = self.share(part, self.me)[...]
+        for device in self.mates:
+            self.push(self.share(part, device[0]), self.plane.at[self.me], 0, device)
+
+    def along(self):
+        self.wait(self.plane.at[pl.ds(0, self.n - 1)], (self.send.at[0], self.recv.at[0]))
+        self.line[self.z] = self.added(self.plane)
+        for device in self.others:
+            self.push(self.line.at[self.z], self.line.at[self.z], 1, device)
+
+    def back(self, out):
+        self.wait(self.line.at[pl.ds(0, self.nz - 1)], (self.send.at[1], self.recv.at[1]))
+        total = self.added(self.line)
+        self.mine[...] = total
+        self.share(out, self.me)[...] = total
+        for device in self.mates:
+            self.push(self.mine, self.share(out, self.me), 2, device)
+
+    def late_spread(self):
+        self.late_plane[self.me] = self.late[...]
+        for device in self.mates:
+            self.push(self.late, self.late_plane.at[self.me], 3, device)
+
+    def late_along(self):
+        self.wait(self.late_plane.at[pl.ds(0, self.n - 1)], (self.send.at[3], self.recv.at[3]))
+        self.late_line[self.z] = self.added(self.late_plane)
+        for device in self.others:
+            self.push(self.late_line.at[self.z], self.late_line.at[self.z], 4, device)
+
+    def close(self):
+        self.wait(self.late_line.at[pl.ds(0, self.nz - 1)], (self.send.at[4], self.recv.at[4]))
+        self.wait(self.plane.at[pl.ds(0, self.n - 1)], (self.send.at[2], self.recv.at[2]))
+        return self.added(self.late_line)
+
+    def added(self, ref):
+        total = ref[0]
+        for at in range(1, ref.shape[0]):
+            total = total + ref[at]
+        return total
+
+
+def backward_kernel(layers, sizes, *refs):
     cot, valid, gain, squares = refs[:4]
     qkv, pt, slope, n1, n2, r1, r2, wqkv, wout, wup, wdown = [
         [ref.at[l] for l in range(layers)] for ref in refs[4:15]
     ]
     q, k, v = [[ref.at[part] for ref in qkv] for part in range(3)]
-    backward_body(layers, cot, valid, gain, squares, q, k, v, pt, slope, n1, n2, r1, r2, wqkv, wout, wup, wdown, *refs[15:])
+    backward_body(
+        layers, sizes, cot, valid, gain, squares, q, k, v, pt, slope, n1, n2, r1, r2, wqkv, wout, wup, wdown, *refs[15:]
+    )
 
 
 def backward_body(
-    layers, cot, valid, gain, squares, q, k, v, pt, slope, n1, n2, r1, r2, wqkv, wout, wup, wdown,
-    dh_out, grads,
+    layers, sizes, cot, valid, gain, squares, q, k, v, pt, slope, n1, n2, r1, r2, wqkv, wout, wup, wdown,
+    dh_out, summed,
     e_buf, x_buf, z_buf, du_buf, dp_buf, do_buf, cot_buf,
     q_buf, k_buf, v_buf, pt_buf, sl_buf, n1_buf, n2_buf,
-    ring_a, ring_b, ring_c, sem_a, sem_b, sem_c, sem_in, sem_out,
+    ring_a, ring_b, ring_c, sem_a, sem_b, sem_c, sem_in, sem_out, *rest,
 ):
     slots, width = e_buf.shape
     ff = du_buf.shape[1]
@@ -95,6 +196,12 @@
     half = slots // 2
     scale = hd ** (-0.5)
     order = list(reversed(range(layers)))
+    fused = len(rest) > 0
+    grads = rest[0] if fused else summed
+    team = None
+    if fused:
+        team = Total(Fabric(sizes), rest[1:])
+        team.greet()
 
     sources = (n2, slope, n1, q, k, v, pt)
     buffers = (n2_buf, sl_buf, n1_buf, q_buf, k_buf, v_buf, pt_buf)
@@ -152,8 +259,17 @@
         s_in, s_out = lax.fori_loop(0, slots // chunk, step, (zero, zero))
         return jnp.sum(s_in, axis=0, keepdims=True), jnp.sum(s_out, axis=0, keepdims=True)
 
+    for l in range(layers):
+        grads[l, 10:13, :] = squares[3 * l : 3 * l + 3, :]
+        grads[l, 13:14, :] = squares[3 * layers : 3 * layers + 1, :]
+        grads[l, 14:16, :] = jnp.zeros((2, width), F32)
+    if fused:
+        grads[order[-1], 0:2, :] = jnp.zeros((2, width), F32)
+
     for step, l in enumerate(order):
         par = step % 2
+        last = step == layers - 1
+        early = fused and last
 
         load(0, l, par).wait()
         s_in, s_out = norm_back(e_buf, x_buf, gain[l, 1:2, :], n2_buf.at[par], r2[l])
@@ -226,13 +342,23 @@
                 dp_buf[rows, pl.ds(pl.multiple_of(2 * width + hp * 2 * hd, 2 * hd), 2 * hd)] = dv.astype(BF)
                 sum_q = sum_q + fold8(dq)
                 sum_v = sum_v + fold8(dv)
-            grads[l, 0:1, cols] = jnp.sum(sum_q, axis=0, keepdims=True)
-            grads[l, 1:2, cols] = jnp.sum(sum_v, axis=0, keepdims=True)
+            terms = team.late if early else grads.at[l]
+            terms[0:1, cols] = jnp.sum(sum_q, axis=0, keepdims=True)
+            terms[1:2, cols] = jnp.sum(sum_v, axis=0, keepdims=True)
             return carry
 
-        lax.fori_loop(0, heads // 2, pair, 0)
+        if early:
+            team.met()
+            team.spread(grads)
+            lax.fori_loop(0, 3, pair, 0)
+            team.along()
+            lax.fori_loop(3, 6, pair, 0)
+            team.back(summed)
+            lax.fori_loop(6, heads // 2, pair, 0)
+            team.late_spread()
+        else:
+            lax.fori_loop(0, heads // 2, pair, 0)
         nc = ring_c.shape[1]
-        last = step == layers - 1
 
         def qkv_body(j, w):
             cols = pl.ds(pl.multiple_of(j * nc, nc), nc)
@@ -240,20 +366,22 @@
             if last:
                 pltpu.make_async_copy(e_buf.at[:, cols], dh_out.at[:, cols], sem_out.at[0]).start()
 
-        rc.run(width // nc, qkv_body)
+        rc.run(width // nc // 2, qkv_body)
+        if early:
+            team.late_along()
+        rc.run(width // nc // 2, qkv_body, width // nc // 2)
         for which in range(7):
             if step + 2 < layers:
                 load(which, order[step + 2], par).start()
-        grads[l, 10:13, :] = squares[3 * l : 3 * l + 3, :]
-        grads[l, 13:14, :] = squares[3 * layers : 3 * layers + 1, :]
-        grads[l, 14:16, :] = jnp.zeros((2, width), F32)
-
+
+    if fused:
+        summed[order[-1], 0:2, :] = team.close()
     for j in range(width // nc):
         cols = pl.ds(j * nc, nc)
         pltpu.make_async_copy(e_buf.at[:, cols], dh_out.at[:, cols], sem_out.at[0]).wait()
 
 
-def backward(cot, valid, gain, squares, kept):
+def backward(sizes, cot, valid, gain, squares, kept):
     slots, width = cot.shape
     layers, heads = kept[1].shape[:2]
     ff = kept[2].shape[2]
@@ -261,8 +389,24 @@
     hbm = pl.BlockSpec(memory_space=pl.ANY)
     vm = pl.BlockSpec(memory_space=pltpu.VMEM)
     ta, tb, tc = min(512, width), min(256, width), min(256, width)
+    team = []
+    params = {}
+    if sizes == KERNEL_MESH:
+        plane, line = 2 * sizes[0] * sizes[1], sizes[2]
+        team = [
+            pltpu.VMEM((layers, 16, width), F32),
+            pltpu.VMEM((plane, layers, 16, width // plane), F32),
+            pltpu.VMEM((line, layers, 16, width // plane), F32),
+            pltpu.VMEM((layers, 16, width // plane), F32),
+            pltpu.VMEM((2, width), F32),
+            pltpu.VMEM((plane, 2, width), F32),
+            pltpu.VMEM((line, 2, width), F32),
+            pltpu.SemaphoreType.DMA((5,)),
+            pltpu.SemaphoreType.DMA((5,)),
+        ]
+        params = dict(collective_id=1, has_side_effects=True)
     return pl.pallas_call(
-        functools.partial(backward_kernel, layers),
+        functools.partial(backward_kernel, layers, sizes),
         out_shape=(
             jax.ShapeDtypeStruct((slots, width), F32),
             jax.ShapeDtypeStruct((layers, 16, width), F32),
@@ -292,30 +436,11 @@
             pltpu.SemaphoreType.DMA((2,)),
             pltpu.SemaphoreType.DMA((2, 7)),
             pltpu.SemaphoreType.DMA((1,)),
-        ],
-        compiler_params=pltpu.CompilerParams(vmem_limit_bytes=67000000),
+        ]
+        + team,
+        compiler_params=pltpu.CompilerParams(vmem_limit_bytes=67000000, **params),
         name="backward",
     )(cot, valid, gain, squares, *kept)
-
-
-class Fabric:
-    def __init__(self, sizes):
-        ny, nx, nz = sizes
-        dp = lax.axis_index("dp")
-        self.size = {"y": ny, "x": nx, "z": nz, "c": 2}
-        self.at = {"z": lax.axis_index("shard"), "c": lax.rem(dp, 2), "x": lax.rem(dp // 2, nx), "y": dp // (2 * nx)}
-
-    def device(self, **moved):
-        at = {**self.at, **moved}
-        return ((at["y"] * self.size["x"] + at["x"]) * 2 + at["c"], at["z"])
-
-    def peers(self, axis):
-        n = self.size[axis]
-        return [lax.rem(self.at[axis] + step, n) for step in range(1, n)]
-
-    def block(self, **moved):
-        at = {**self.at, **moved}
-        return ((at["y"] * self.size["x"] + at["x"]) * 2 + at["c"]) * self.size["z"] + at["z"]
 
 
 class Relay:
@@ -423,7 +548,7 @@
             pl.when(self.inner)(lambda piece=piece: self.wait(self.send.at[2 * t + piece, 2], 8))
 
 
-LEADS = (9, 7, 5, 4, 2, 1)
+LEADS = (12, 10, 8, 6, 4, 2)
 
 
 def forward_kernel(layers, sizes, *refs):
@@ -726,64 +851,6 @@
     return result[0], result[1], list(result[2:])
 
 
-def total_kernel(sizes, part, out, z_buf, acc, send, recv):
-    fab = Fabric(sizes)
-    barrier = pltpu.get_barrier_semaphore()
-    around = [fab.device(**{axis: peer}) for axis in ("c", "z", "x", "y") for peer in fab.peers(axis)]
-    for device in around:
-        pl.semaphore_signal(barrier, inc=1, device_id=device, device_id_type=pl.DeviceIdType.MESH)
-    pl.semaphore_wait(barrier, len(around))
-    sem = 0
-    slot = 0
-    acc[...] = part[...]
-    for axis in ("c", "z", "x", "y"):
-        n = fab.size[axis]
-        me = fab.at[axis]
-        copies = []
-        z_buf[slot + me] = acc[...]
-        for peer in fab.peers(axis):
-            copies.append(
-                pltpu.make_async_remote_copy(
-                    src_ref=z_buf.at[slot + me],
-                    dst_ref=z_buf.at[slot + me],
-                    send_sem=send.at[sem],
-                    recv_sem=recv.at[sem],
-                    device_id=fab.device(**{axis: peer}),
-                    device_id_type=pl.DeviceIdType.MESH,
-                )
-            )
-            copies[-1].start()
-            sem += 1
-        for copy in copies:
-            copy.wait()
-        total = z_buf[slot]
-        for at in range(1, n):
-            total = total + z_buf[slot + at]
-        acc[...] = total
-        slot += n
-    out[...] = acc[...]
-
-
-def total_of(sizes, part):
-    vm = pl.BlockSpec(memory_space=pltpu.VMEM)
-    steps = sum(n - 1 for n in sizes) + 1
-    slots = sum(sizes) + 2
-    return pl.pallas_call(
-        functools.partial(total_kernel, sizes),
-        out_shape=jax.ShapeDtypeStruct(part.shape, F32),
-        in_specs=[vm],
-        out_specs=vm,
-        scratch_shapes=[
-            pltpu.VMEM((slots,) + part.shape, F32),
-            pltpu.VMEM(part.shape, F32),
-            pltpu.SemaphoreType.DMA((steps,)),
-            pltpu.SemaphoreType.DMA((steps,)),
-        ],
-        compiler_params=pltpu.CompilerParams(vmem_limit_bytes=32 << 20, collective_id=1, has_side_effects=True),
-        name="total",
-    )(part)
-
-
 def normalize(stream, gain_row, shift_row):
     mean_row = jnp.mean(stream, axis=-1, keepdims=True)
     centred = stream - mean_row
@@ -843,13 +910,14 @@
     def turn(a, by):
         return lax.dynamic_slice_in_dim(jnp.concatenate([a, a], axis=0), by, slots, axis=0)
 
-    run = functools.partial(forward, sizes) if sizes == (2, 2, 4) else forward_apart
+    run = functools.partial(forward, sizes) if sizes == KERNEL_MESH else forward_apart
     act, squares, kept = run(
         turn(tokens, shift), valid[:, None], valid[None, :], ln_gain, bias_qv, bias_out, ln_bias, bias_up, bias_down,
         w_qkv, w_out, w_up, w_down,
     )
-    dh, part = backward(turn(cotangent, shift), valid[:, None], ln_gain, squares, kept)
-    whole = total_of(sizes, part)
+    dh, whole = backward(sizes, turn(cotangent, shift), valid[:, None], ln_gain, squares, kept)
+    if sizes != KERNEL_MESH:
+        whole = lax.psum(whole, AXES)
     back = lax.rem(slots - shift, slots)
     return (
         turn(act, back),

time: 340 us -> 308 us (0.906)
  Pallas kernels: 318 us -> 287 us
    pallas_call x2 -> x1, Pallas kernels: 100 us -> 78.1 us  [backward(): pl.pallas_call(functools.partial(backward_kernel, layers, sizes), out_sha...]
    pallas_call x1, Pallas kernels: 218 us -> 208 us  [forward(): pl.pallas_call(functools.partial(forward_kernel, layers, sizes), out_shap...]
where the time goes in v1:
time: 308 us; the launch traced here: 307 us
  Pallas kernels  287 us (93%)
  other arithmetic  13.8 us (4%)
  local copies, waits for them, and re-layouts  3.81 us (1%)
  between operations  3.28 us (1%)
    pallas_call x1, Pallas kernels, forward(): pl.pallas_call(functools.partial(forward_kernel, layers, sizes), out_shap...  208 us
    pallas_call x1, Pallas kernels, backward(): pl.pallas_call(functools.partial(backward_kernel, layers, sizes), out_sha...  78.1 us
    concatenate x3, other arithmetic, turn(): jnp.concatenate([a, a], axis=0)  11.6 us

profile of v1, /device:TPU:0, one launch (start us, length us, event | category | flops | bytes accessed | tf_op | source)
XLA Modules:
  0.0 307.5 jit_solution(16827921491048073394)
XLA Ops:
  0.6 1.3 fusion.10
  4.6 0.6 compare_convert_fusion.refs_2_
  5.1 0.8 fusion.6.refs_1_
  5.9 4.6 %fusion.1 = (bf16[512,1024]{1,0:T(8,128)(2,1)}, bf16[512,1024]{1,0:T(8,128)(2,1)}) fusion(s32[]{:T(128)S(6)} %select_n.13, bf16[512,1024]{1,0:T(8,128)(2,1)} %param.25, bf16[512,1024]{1,0:T(8,128)(2,1)} %param.13), kind=kLoop, calls=%fused_computation.9 | loop fusion | flops 4194304 | bytes 4194308 | tf_op jit(solution)/shard_map/concatenate | solution.py:911
  10.5 208.5 %forward.1 = (bf16[512,1024]{1,0:T(8,128)(2,1)}, f32[8,1024]{1,0:T(8,128)}, bf16[2,3,512,1024]{3,2,1,0:T(8,128)(2,1)}, bf16[2,16,2,256,256]{4,3,2,1,0:T(8,128)(2...) custom-call(bf16[512,1024]{1,0:T(8,128)(2,1)} %get-tuple-element.45., ...), custom_call_target="tpu_custom_call" | custom-call | tf_op jit(solution)/shard_map/forward/pallas_call | solution.py:821
  219.0 3.2 %fusion.2 = bf16[512,1024]{1,0:T(8,128)(2,1)} fusion(s32[]{:T(128)S(6)} %select_n.14, bf16[512,1024]{1,0:T(8,128)(2,1)} %get-tuple-element.23), kind=kLoop, calls=%fused_computation.10 | loop fusion | flops 2097152 | bytes 2097156 | tf_op jit(solution)/shard_map/concatenate | solution.py:911
  222.2 78.1 %backward.1 = (f32[512,1024]{1,0:T(8,128)}, f32[2,16,1024]{2,1,0:T(8,128)}) custom-call(bf16[512,1024]{1,0:T(8,128)(2,1)} %get-tuple-element.44.refs_0_, f32[512,1]{1,0:T(8,128)} %fusion.6.refs_1_, f32[2,2,1024]{2,1,0:T(2,128)} %refs_2_.1, f32[8,1024]{1,0:T(8,128)} %get-tuple-element.24.refs_3_, bf16[2,3,512,1024]{3,2,1,0:T(8,128)(2,1)} %get-tuple-element.25.refs_4_, ...), custom_call_target="tpu_custom_call" | custom-call | tf_op jit(solution)/shard_map/backward/pallas_call | solution.py:408
  300.3 0.0 copy-start
  300.3 3.8 %fusion = f32[512,1024]{1,0:T(8,128)} fusion(s32[]{:T(128)S(6)} %select_n.14, f32[512,1024]{1,0:T(8,128)} %get-tuple-element.36), kind=kLoop, calls=%fused_computation.2 | loop fusion | flops 524288 | bytes 4194308 | tf_op jit(solution)/shard_map/concatenate | solution.py:911
  304.1 0.0 copy-done
  304.1 0.1 multiply_reduce_fusion
  304.2 0.1 slice_reduce_fusion
  304.3 0.6 divide_sqrt_fusion
  305.0 0.6 copy.26
  305.6 0.6 copy.27
  306.2 0.6 fusion.9
  306.8 0.6 copy.23
  (2 shorter events, 0.0 us)
Async XLA Ops:
  300.3 3.8 %copy-start = (f32[2,16,1024]{2,1,0:T(8,128)S(1)}, f32[2,16,1024]{2,1,0:T(8,128)}, u32[]{:S(2)}) copy-start(f32[2,16,1024]{2,1,0:T(8,128)} %get-tuple-element.37) | copy-start | bytes 393220

commit v2 on v1

--- a/solution.py
+++ b/solution.py
@@ -172,18 +172,18 @@
 
 
 def backward_kernel(layers, sizes, *refs):
-    cot, valid, gain, squares = refs[:4]
+    cot, gain, squares = refs[:3]
     qkv, pt, slope, n1, n2, r1, r2, wqkv, wout, wup, wdown = [
-        [ref.at[l] for l in range(layers)] for ref in refs[4:15]
+        [ref.at[l] for l in range(layers)] for ref in refs[3:14]
     ]
     q, k, v = [[ref.at[part] for ref in qkv] for part in range(3)]
     backward_body(
-        layers, sizes, cot, valid, gain, squares, q, k, v, pt, slope, n1, n2, r1, r2, wqkv, wout, wup, wdown, *refs[15:]
+        layers, sizes, cot, gain, squares, q, k, v, pt, slope, n1, n2, r1, r2, wqkv, wout, wup, wdown, *refs[14:]
     )
 
 
 def backward_body(
-    layers, sizes, cot, valid, gain, squares, q, k, v, pt, slope, n1, n2, r1, r2, wqkv, wout, wup, wdown,
+    layers, sizes, cot, gain, squares, q, k, v, pt, slope, n1, n2, r1, r2, wqkv, wout, wup, wdown,
     dh_out, summed,
     e_buf, x_buf, z_buf, du_buf, dp_buf, do_buf, cot_buf,
     q_buf, k_buf, v_buf, pt_buf, sl_buf, n1_buf, n2_buf,
@@ -234,12 +234,12 @@
     chunk = 32
     cot_copy.wait()
 
-    def mask_cot(c, carry):
+    def widen(c, carry):
         rows = pl.ds(pl.multiple_of(c * chunk, chunk), chunk)
-        e_buf[rows, :] = cot_buf[rows, :].astype(F32) * valid[rows, :]
+        e_buf[rows, :] = cot_buf[rows, :].astype(F32)
         return carry
 
-    lax.fori_loop(0, slots // chunk, mask_cot, 0)
+    lax.fori_loop(0, slots // chunk, widen, 0)
 
     def norm_back(src, dst, gain_row, n_ref, r_ref):
         def step(c, carry):
@@ -381,7 +381,7 @@
         pltpu.make_async_copy(e_buf.at[:, cols], dh_out.at[:, cols], sem_out.at[0]).wait()
 
 
-def backward(sizes, cot, valid, gain, squares, kept):
+def backward(sizes, cot, gain, squares, kept):
     slots, width = cot.shape
     layers, heads = kept[1].shape[:2]
     ff = kept[2].shape[2]
@@ -411,7 +411,7 @@
             jax.ShapeDtypeStruct((slots, width), F32),
             jax.ShapeDtypeStruct((layers, 16, width), F32),
         ),
-        in_specs=[hbm, vm, vm, vm] + [hbm] * 5 + [vm] * 2 + [hbm] * 4,
+        in_specs=[hbm, vm, vm] + [hbm] * 5 + [vm] * 2 + [hbm] * 4,
         out_specs=(hbm, vm),
         scratch_shapes=[
             pltpu.VMEM((slots, width), F32),
@@ -440,7 +440,7 @@
         + team,
         compiler_params=pltpu.CompilerParams(vmem_limit_bytes=67000000, **params),
         name="backward",
-    )(cot, valid, gain, squares, *kept)
+    )(cot, gain, squares, *kept)
 
 
 class Relay:
@@ -552,13 +552,13 @@
 
 
 def forward_kernel(layers, sizes, *refs):
-    (tok, vcol, vrow, gain, b_qv, b_out, b_ln, b_up, b_down, s_qkv, s_out, s_up, s_down) = refs[:13]
-    (act, squares, qkv_o, pt_o, sl_o, n1_o, n2_o, r1_o, r2_o, f_qkv, f_out, f_up, f_down) = refs[13:26]
+    (lens, tok, cot, gain, b_qv, b_out, b_ln, b_up, b_down, s_qkv, s_out, s_up, s_down) = refs[:13]
+    (act, squares, back, cot_o, qkv_o, pt_o, sl_o, n1_o, n2_o, r1_o, r2_o, f_qkv, f_out, f_up, f_down) = refs[13:28]
     (
         h_buf, hb_buf, qkv_buf, mix_buf, gu_buf, f_buf, pt_buf, sl_buf, n_buf,
-        ring_w, ring_t, own_qkv, own_out, own_up, own_down,
+        ring_w, ring_t, own_qkv, own_out, own_up, own_down, turn, vcol, vrow,
         sem_send, sem_recv, sem_own, sem_ring, sem_save,
-    ) = refs[26:]
+    ) = refs[28:]
     slots, width = tok.shape
     ff = gu_buf.shape[1]
     heads = pt_buf.shape[0]
@@ -571,6 +571,7 @@
     shards = ((s_qkv, own_qkv, f_qkv), (s_out, own_out, f_out), (s_up, own_up, f_up), (s_down, own_down, f_down))
     for at, (src, buf, _) in enumerate(shards):
         pltpu.make_async_copy(src, buf, sem_own.at[at]).start()
+    pltpu.make_async_copy(cot, mix_buf, sem_save.at[3]).start()
     barrier = pltpu.get_barrier_semaphore()
     around = [fab.device(**{axis: peer}) for axis in ("z", "x", "y", "c") for peer in fab.peers(axis)]
     for device in around:
@@ -721,7 +722,7 @@
 
             @pl.when(part == downs - 1)
             def _():
-                free(n_buf.at[1], n2_o.at[0], 5, later)
+                free(n_buf.at[1], n2_o.at[0], 5, True)
                 _, s_f = norm(l, 1, b_down[pl.ds(l, 1), :], h_buf, f_buf, n_buf.at[1], r2_o.at[l])
                 squares[pl.ds(3 * l + 2, 1), :] = jnp.sum(s_f, axis=0, keepdims=True)
                 save(n_buf.at[1], n2_o.at[l], 5)
@@ -742,8 +743,7 @@
         slot = lax.rem(t, 2)
         pltpu.make_async_copy(f_out.at[0], ring_w.at[slot], sem_ring.at[slot]).wait()
 
-    early = LEADS[0] - LEADS[1]
-    for t in range(early):
+    for t in range(LEADS[0] - LEADS[1]):
         relay.stage(0, jnp.int32(t))
     for at, (src, buf, _) in enumerate(shards):
         pltpu.make_async_copy(src, buf, sem_own.at[at]).wait()
@@ -755,13 +755,40 @@
             placed.append(pltpu.make_async_copy(buf.at[l], dst, sem_own.at[4 + at * layers + l]))
             placed[-1].start()
 
-    def widen(c, carry):
+    first, second = lens[0, 0], lens[0, 1]
+    shift = jnp.where(first == half, 0, first)
+    back[0] = slots - shift
+
+    def source(slot):
+        return jnp.where(slot + shift >= slots, slot + shift - slots, slot + shift)
+
+    vcol[...] = (source(lax.broadcasted_iota(jnp.int32, (slots, 1), 0)) < first + second).astype(F32)
+    vrow[...] = (source(lax.broadcasted_iota(jnp.int32, (1, slots), 1)) < first + second).astype(F32)
+
+    def turning(c, carry):
         rows = rows_of(c)
-        h_buf[rows, :] = tok[rows, :].astype(F32)
-        hb_buf[rows, :] = tok[rows, :]
+        slot = lax.broadcasted_iota(jnp.int32, (chunk, slots), 0) + c * chunk
+        turn[rows, :] = (source(slot) == lax.broadcasted_iota(jnp.int32, (chunk, slots), 1)).astype(F32).astype(BF)
         return carry
 
-    lax.fori_loop(0, steps, widen, 0)
+    lax.fori_loop(0, steps, turning, 0)
+
+    def turned(dst, src):
+        def body(j, carry):
+            cols = pl.ds(pl.multiple_of(j * 256, 256), 256)
+            dst(cols, nn(turn[...], src[:, cols]))
+            return carry
+
+        lax.fori_loop(0, width // 256, body, 0)
+
+    def put_tokens(cols, t):
+        h_buf[:, cols] = t
+        hb_buf[:, cols] = t.astype(BF)
+
+    def put_cotangent(cols, t):
+        n_buf[1, :, cols] = (t * vcol[...]).astype(BF)
+
+    turned(put_tokens, tok)
     for copy in placed:
         copy.wait()
 
@@ -769,6 +796,13 @@
         at = i - LEADS[1]
         for s, lead in enumerate(LEADS):
             relay.stage(s, at + lead)
+
+        @pl.when(i == 4)
+        def _():
+            pltpu.make_async_copy(cot, mix_buf, sem_save.at[3]).wait()
+            turned(put_cotangent, mix_buf)
+            save(n_buf.at[1], cot_o, 5)
+
         pl.when(jnp.logical_and(at >= 1, at <= total))(lambda: ring_wait(at - 1))
 
         @pl.when(jnp.logical_and(at >= 0, at < total))
@@ -794,7 +828,7 @@
     pltpu.make_async_copy(hb_buf, act, sem_own.at[0]).wait()
 
 
-def forward(sizes, tokens, vcol, vrow, gain, b_qv, b_out, b_ln, b_up, b_down, s_qkv, s_out, s_up, s_down):
+def forward(sizes, lengths, tokens, cotangent, gain, b_qv, b_out, b_ln, b_up, b_down, s_qkv, s_out, s_up, s_down):
     slots, width = tokens.shape
     layers = s_qkv.shape[0]
     ff = s_up.shape[2]
@@ -806,6 +840,8 @@
     outs = [
         ((slots, width), BF, hbm),
         ((8, width), F32, vm),
+        ((1,), jnp.int32, pl.BlockSpec(memory_space=pltpu.SMEM)),
+        ((slots, width), BF, hbm),
         ((layers, 3, slots, width), BF, hbm),
         ((layers, HEADS, 2, half, half), BF, hbm),
         ((layers, slots, ff), BF, hbm),
@@ -821,7 +857,7 @@
     result = pl.pallas_call(
         functools.partial(forward_kernel, layers, sizes),
         out_shape=tuple(jax.ShapeDtypeStruct(shape, kind) for shape, kind, _ in outs),
-        in_specs=[vm] * 9 + [hbm] * 4,
+        in_specs=[pl.BlockSpec(memory_space=pltpu.SMEM), vm, hbm] + [vm] * 6 + [hbm] * 4,
         out_specs=tuple(spec for _, _, spec in outs),
         scratch_shapes=[
             pltpu.VMEM((slots, width), F32),
@@ -839,6 +875,9 @@
             pltpu.VMEM(s_out.shape, BF),
             pltpu.VMEM(s_up.shape, BF),
             pltpu.VMEM(s_down.shape, BF),
+            pltpu.VMEM((slots, slots), BF),
+            pltpu.VMEM((slots, 1), F32),
+            pltpu.VMEM((1, slots), F32),
             pltpu.SemaphoreType.DMA((2 * chunks, 5)),
             pltpu.SemaphoreType.DMA((2 * chunks, 5)),
             pltpu.SemaphoreType.DMA((4 + 4 * layers,)),
@@ -847,8 +886,8 @@
         ],
         compiler_params=pltpu.CompilerParams(vmem_limit_bytes=62 << 20, collective_id=0, has_side_effects=True),
         name="forward",
-    )(tokens, vcol, vrow, gain, b_qv, b_out, b_ln, b_up, b_down, s_qkv, s_out, s_up, s_down)
-    return result[0], result[1], list(result[2:])
+    )(lengths, tokens, cotangent, gain, b_qv, b_out, b_ln, b_up, b_down, s_qkv, s_out, s_up, s_down)
+    return result[0], result[1], result[2], result[3], list(result[4:])
 
 
 def normalize(stream, gain_row, shift_row):
@@ -860,8 +899,17 @@
     return normed * gain_row + shift_row, normed, inv_std
 
 
-def forward_apart(tokens, vcol, vrow, gain, b_qv, b_out, b_ln, b_up, b_down, *shards):
+def turned_by(a, by):
+    return lax.dynamic_slice_in_dim(jnp.concatenate([a, a], axis=0), by, a.shape[0], axis=0)
+
+
+def forward_apart(lengths, tokens, cotangent, gain, b_qv, b_out, b_ln, b_up, b_down, *shards):
     slots, width = tokens.shape
+    shift = jnp.where(lengths[0, 0] == slots // 2, 0, lengths[0, 0])
+    place = lax.rem(jnp.arange(slots, dtype=jnp.int32) + shift, slots)
+    vcol = (place < lengths[0, 0] + lengths[0, 1]).astype(F32)[:, None]
+    tokens = turned_by(tokens, shift)
+    masked = turned_by(cotangent, shift) * vcol.astype(BF)
     layers = b_out.shape[0]
     half = slots // 2
     hd = width // HEADS
@@ -893,7 +941,7 @@
         kept.append((jnp.stack([q, k, v]), pt, slope, n1.astype(BF), n2.astype(BF), r1, r2, *mats))
         stream = nxt
     here = jnp.broadcast_to(jnp.sum(vcol), (width,))
-    return stream.astype(BF), jnp.stack(squares + [here] * (8 - 3 * layers)), [jnp.stack(a) for a in zip(*kept)]
+    return stream.astype(BF), jnp.stack(squares + [here] * (8 - 3 * layers)), (slots - shift)[None], masked, [jnp.stack(a) for a in zip(*kept)]
 
 
 def local(
@@ -901,27 +949,17 @@
 ):
     slots, width = tokens.shape
     layers = w_qkv.shape[0]
-    half = slots // 2
-    first, second = lengths[0, 0], lengths[0, 1]
-    shift = jnp.where(first == half, 0, first)
-    place = lax.rem(jnp.arange(slots, dtype=jnp.int32) + shift, slots)
-    valid = (place < first + second).astype(F32)
-
-    def turn(a, by):
-        return lax.dynamic_slice_in_dim(jnp.concatenate([a, a], axis=0), by, slots, axis=0)
-
     run = functools.partial(forward, sizes) if sizes == KERNEL_MESH else forward_apart
-    act, squares, kept = run(
-        turn(tokens, shift), valid[:, None], valid[None, :], ln_gain, bias_qv, bias_out, ln_bias, bias_up, bias_down,
-        w_qkv, w_out, w_up, w_down,
+    act, squares, back, cot, kept = run(
+        lengths, tokens, cotangent, ln_gain, bias_qv, bias_out, ln_bias, bias_up, bias_down, w_qkv, w_out, w_up, w_down
     )
-    dh, whole = backward(sizes, turn(cotangent, shift), valid[:, None], ln_gain, squares, kept)
+    dh, whole = backward(sizes, cot, ln_gain, squares, kept)
     if sizes != KERNEL_MESH:
         whole = lax.psum(whole, AXES)
-    back = lax.rem(slots - shift, slots)
+    back = back[0].astype(jnp.uint32)
     return (
-        turn(act, back),
-        turn(dh, back),
+        turned_by(act, back),
+        turned_by(dh, back),
         whole[:, 0:2],
         whole[:, 2],
         whole[:, 3:5],

time: 308 us -> 297 us (0.964)
  other arithmetic: 13.8 us -> 7.82 us
    concatenate x3 -> x2, other arithmetic: 11.6 us -> 6.98 us  [turned_by(): jnp.concatenate([a, a], axis=0)]
where the time goes in v2:
time: 297 us
  Pallas kernels  286 us (96%)
  other arithmetic  7.82 us (3%)
    pallas_call x1, Pallas kernels, forward(): pl.pallas_call(functools.partial(forward_kernel, layers, sizes), out_shap...  209 us
    pallas_call x1, Pallas kernels, backward(): pl.pallas_call(functools.partial(backward_kernel, layers, sizes), out_sha...  77 us
    concatenate x2, other arithmetic, turned_by(): jnp.concatenate([a, a], axis=0)  6.98 us

profile of v2, /device:TPU:0, one launch (start us, length us, event | category | flops | bytes accessed | tf_op | source)
XLA Modules:
  0.0 296.7 jit_solution(10774686434459909730)
XLA Ops:
  0.6 208.7 %forward.1 = (bf16[512,1024]{1,0:T(8,128)(2,1)}, f32[8,1024]{1,0:T(8,128)}, s32[1]{0:T(128)}, bf16[512,1024]{1,0:T(8,128)(2,1)}, bf16[2,3,512,1024]{3,2,1,0:T(8,...) custom-call(s32[1,2]{1,0:T(1,128)} %refs_0_.1, ...), custom_call_target="tpu_custom_call" | custom-call | tf_op jit(solution)/shard_map/forward/pallas_call | solution.py:857
  209.9 3.2 %fusion.1 = bf16[512,1024]{1,0:T(8,128)(2,1)} fusion(u32[]{:T(128)} %bitcast, bf16[512,1024]{1,0:T(8,128)(2,1)} %get-tuple-element.25), kind=kLoop, calls=%fused_computation.5 | loop fusion | flops 2097152 | bytes 2097156 | tf_op jit(solution)/shard_map/concatenate | solution.py:903
  213.1 77.0 %backward.1 = (f32[512,1024]{1,0:T(8,128)}, f32[2,16,1024]{2,1,0:T(8,128)}) custom-call(bf16[512,1024]{1,0:T(8,128)(2,1)} %get-tuple-element.27.refs_0_, f32[2,2,1024]{2,1,0:T(2,128)} %refs_1_.3, f32[8,1024]{1,0:T(8,128)} %get-tuple-element.28.refs_2_, bf16[2,3,512,1024]{3,2,1,0:T(8,128)(2,1)} %get-tuple-element.29.refs_3_, ...), custom_call_target="tpu_custom_call" | custom-call | tf_op jit(solution)/shard_map/backward/pallas_call | solution.py:408
  290.1 0.0 copy-start
  290.1 3.8 %fusion = f32[512,1024]{1,0:T(8,128)} fusion(u32[]{:T(128)} %bitcast, f32[512,1024]{1,0:T(8,128)} %get-tuple-element.40), kind=kLoop, calls=%fused_computation.2 | loop fusion | flops 524288 | bytes 4194308 | tf_op jit(solution)/shard_map/concatenate | solution.py:903
  293.9 0.0 copy-done
  293.9 0.1 multiply_reduce_fusion
  294.0 0.1 slice_reduce_fusion
  294.1 0.6 divide_sqrt_fusion
  294.8 0.6 copy_bitcast_fusion
  295.4 0.6 fusion.3
  296.0 0.6 copy.23
  (2 shorter events, 0.0 us)
Async XLA Ops:
  290.1 3.8 %copy-start = (f32[2,16,1024]{2,1,0:T(8,128)S(1)}, f32[2,16,1024]{2,1,0:T(8,128)}, u32[]{:S(2)}) copy-start(f32[2,16,1024]{2,1,0:T(8,128)} %get-tuple-element.41) | copy-start | bytes 393220

commit v3 on v2

--- a/solution.py
+++ b/solution.py
@@ -497,8 +497,9 @@
                     pl.when(jnp.logical_not(self.inner))(
                         lambda piece=piece: self.wait(self.recv.at[2 * t + piece, 2], 4)
                     )
+                    self.wait(self.recv.at[2 * t + piece, 5], 4)
                 elif s == 5:
-                    self.wait(self.recv.at[2 * t + piece, 3], 8)
+                    self.wait(self.recv.at[2 * t + piece, 3], 4)
 
             def act(l, own, full, rows, cols, piece):
                 u, v = (("x", "y"), ("y", "x"))[piece]
@@ -510,7 +511,11 @@
                     for first, blocks in runs:
                         self.push(t, piece, sem, device, view(first, blocks), view(first, blocks))
 
-                far = [(fab.block(**{u: each, "z": self.other}), 2) for each in range(2)]
+                def runs(z, **moved):
+                    return [(fab.block(**{u: each, "z": z, **moved}), 2) for each in range(2)]
+
+                across = fab.device(**{v: 1 - at[v]})
+                beyond = {v: 1 - at[v]}
                 if s == 0:
                     mine = view(fab.block(), 1)
                     self.push(t, piece, 0, fab.device(z=self.mate), own.at[l, :, cols], mine)
@@ -519,21 +524,27 @@
                     out(1, fab.device(**{u: 1 - at[u]}), [(fab.block(z=self.pair), 2)])
                     out(4, partner, [(fab.block(z=self.mate), 1)])
                 elif s == 2:
-                    near = [(fab.block(**{u: each, "z": self.pair}), 2) for each in range(2)]
-                    pl.when(self.inner)(lambda: out(2, fab.device(z=3 - at["z"]), near))
+                    pl.when(self.inner)(lambda: out(2, fab.device(z=3 - at["z"]), runs(self.pair)))
+                    out(5, across, runs(self.pair))
                     out(4, partner, [(fab.block(**{u: 1 - at[u], "z": self.pair}), 2)])
                 elif s == 3:
 
                     @pl.when(self.inner)
                     def _():
-                        out(2, fab.device(z=self.mate), far)
-                        out(4, partner, far)
+                        out(2, fab.device(z=self.mate), runs(self.other))
+                        out(3, across, runs(self.other))
+                        out(4, partner, runs(self.other))
 
                 elif s == 4:
-                    out(3, fab.device(**{v: 1 - at[v]}), [(fab.block(**{u: each, "z": 0}), 4) for each in range(2)])
-                    pl.when(jnp.logical_not(self.inner))(lambda: out(4, partner, far))
+
+                    @pl.when(jnp.logical_not(self.inner))
+                    def _():
+                        out(3, across, runs(self.other))
+                        out(4, partner, runs(self.other))
+
+                    out(4, partner, runs(self.pair, **beyond))
                 else:
-                    out(4, partner, [(fab.block(**{v: 1 - at[v], u: each, "z": 0}), 4) for each in range(2)])
+                    out(4, partner, runs(self.other, **beyond))
 
             self.each(t, act)
 
@@ -543,12 +554,12 @@
 
     def drain(self, t):
         for piece in range(2):
-            for sem, blocks in ((0, 1), (1, 2), (3, 8), (4, 16)):
+            for sem, blocks in ((0, 1), (1, 2), (3, 4), (4, 16), (5, 4)):
                 self.wait(self.send.at[2 * t + piece, sem], blocks)
             pl.when(self.inner)(lambda piece=piece: self.wait(self.send.at[2 * t + piece, 2], 8))
 
 
-LEADS = (12, 10, 8, 6, 4, 2)
+LEADS = (11, 9, 7, 5, 3, 1)
 
 
 def forward_kernel(layers, sizes, *refs):
@@ -878,8 +889,8 @@
             pltpu.VMEM((slots, slots), BF),
             pltpu.VMEM((slots, 1), F32),
             pltpu.VMEM((1, slots), F32),
-            pltpu.SemaphoreType.DMA((2 * chunks, 5)),
-            pltpu.SemaphoreType.DMA((2 * chunks, 5)),
+            pltpu.SemaphoreType.DMA((2 * chunks, 6)),
+            pltpu.SemaphoreType.DMA((2 * chunks, 6)),
             pltpu.SemaphoreType.DMA((4 + 4 * layers,)),
             pltpu.SemaphoreType.DMA((2,)),
             pltpu.SemaphoreType.DMA((8,)),

time: 297 us -> 291 us (0.980)
  Pallas kernels: 286 us -> 280 us
    pallas_call x1, Pallas kernels: 209 us -> 203 us  [forward(): pl.pallas_call(functools.partial(forward_kernel, layers, sizes), out_shap...]
where the time goes in v3:
time: 291 us
  Pallas kernels  280 us (96%)
  other arithmetic  7.82 us (3%)
    pallas_call x1, Pallas kernels, forward(): pl.pallas_call(functools.partial(forward_kernel, layers, sizes), out_shap...  203 us
    pallas_call x1, Pallas kernels, backward(): pl.pallas_call(functools.partial(backward_kernel, layers, sizes), out_sha...  77.3 us
    concatenate x2, other arithmetic, turned_by(): jnp.concatenate([a, a], axis=0)  6.98 us

profile of v3, /device:TPU:0, one launch (start us, length us, event | category | flops | bytes accessed | tf_op | source)
XLA Modules:
  0.0 290.9 jit_solution(3554564365950226171)
XLA Ops:
  0.6 202.6 %forward.1 = (bf16[512,1024]{1,0:T(8,128)(2,1)}, f32[8,1024]{1,0:T(8,128)}, s32[1]{0:T(128)}, bf16[512,1024]{1,0:T(8,128)(2,1)}, bf16[2,3,512,1024]{3,2,1,0:T(8,...) custom-call(s32[1,2]{1,0:T(1,128)} %refs_0_.1, ...), custom_call_target="tpu_custom_call" | custom-call | tf_op jit(solution)/shard_map/forward/pallas_call | solution.py:868
  203.8 3.2 %fusion.1 = bf16[512,1024]{1,0:T(8,128)(2,1)} fusion(u32[]{:T(128)} %bitcast, bf16[512,1024]{1,0:T(8,128)(2,1)} %get-tuple-element.25), kind=kLoop, calls=%fused_computation.5 | loop fusion | flops 2097152 | bytes 2097156 | tf_op jit(solution)/shard_map/concatenate | solution.py:914
  207.0 77.3 %backward.1 = (f32[512,1024]{1,0:T(8,128)}, f32[2,16,1024]{2,1,0:T(8,128)}) custom-call(bf16[512,1024]{1,0:T(8,128)(2,1)} %get-tuple-element.27.refs_0_, f32[2,2,1024]{2,1,0:T(2,128)} %refs_1_.3, f32[8,1024]{1,0:T(8,128)} %get-tuple-element.28.refs_2_, bf16[2,3,512,1024]{3,2,1,0:T(8,128)(2,1)} %get-tuple-element.29.refs_3_, ...), custom_call_target="tpu_custom_call" | custom-call | tf_op jit(solution)/shard_map/backward/pallas_call | solution.py:408
  284.4 0.0 copy-start
  284.4 3.8 %fusion = f32[512,1024]{1,0:T(8,128)} fusion(u32[]{:T(128)} %bitcast, f32[512,1024]{1,0:T(8,128)} %get-tuple-element.40), kind=kLoop, calls=%fused_computation.2 | loop fusion | flops 524288 | bytes 4194308 | tf_op jit(solution)/shard_map/concatenate | solution.py:914
  288.2 0.0 copy-done
  288.2 0.1 multiply_reduce_fusion
  288.3 0.1 slice_reduce_fusion
  288.4 0.6 divide_sqrt_fusion
  289.0 0.6 copy_bitcast_fusion
  289.7 0.6 fusion.3
  290.3 0.6 copy.23
  (2 shorter events, 0.0 us)
Async XLA Ops:
  284.4 3.8 %copy-start = (f32[2,16,1024]{2,1,0:T(8,128)S(1)}, f32[2,16,1024]{2,1,0:T(8,128)}, u32[]{:S(2)}) copy-start(f32[2,16,1024]{2,1,0:T(8,128)} %get-tuple-element.41) | copy-start | bytes 393220

commit v4 on v3

--- a/solution.py
+++ b/solution.py
@@ -222,14 +222,6 @@
     ra, rb, rc = Ring(ring_a, sem_a, seg_a), Ring(ring_b, sem_b, seg_b), Ring(ring_c, sem_c, seg_c)
     ra.prime()
     load(1, order[0], 0).start()
-    rb.prime()
-    for which in range(2, 7):
-        load(which, order[0], 0).start()
-    rc.prime()
-    for which in range(7):
-        for step, l in enumerate(order[1:], 1):
-            if step < 2:
-                load(which, l, step).start()
 
     chunk = 32
     cot_copy.wait()
@@ -276,6 +268,9 @@
         grads[l, 4:5, :] = s_in
         grads[l, 9:10, :] = s_out
 
+        if step == 0:
+            rb.prime()
+            load(2, l, par).start()
         load(1, l, par).wait()
         wide = ring_a.shape[1]
 
@@ -288,6 +283,10 @@
             grads[l, pl.ds(5 + j // per, 1), pl.ds(pl.multiple_of(lax.rem(j, per) * wide, wide), wide)] = part
 
         ra.run(ff // wide, down_body)
+        if step == 0:
+            for which in range(3, 7):
+                load(which, l, par).start()
+            rc.prime()
         nb = ring_b.shape[1]
 
         def up_body(j, w):
@@ -295,6 +294,9 @@
             x_buf[:, cols] = x_buf[:, cols] + nt(du_buf[...], w)
 
         rb.run(width // nb, up_body)
+        if step + 1 < layers:
+            for which in range(7):
+                load(which, order[step + 1], 1 - par).start()
 
         load(2, l, par).wait()
         s_in, s_out = norm_back(x_buf, x_buf, gain[l, 0:1, :], n1_buf.at[par], r1[l])
@@ -370,9 +372,6 @@
         if early:
             team.late_along()
         rc.run(width // nc // 2, qkv_body, width // nc // 2)
-        for which in range(7):
-            if step + 2 < layers:
-                load(which, order[step + 2], par).start()
 
     if fused:
         summed[order[-1], 0:2, :] = team.close()
@@ -428,12 +427,12 @@
             pltpu.VMEM((2, slots, ff), BF),
             pltpu.VMEM((2, slots, width), BF),
             pltpu.VMEM((2, slots, width), BF),
-            pltpu.VMEM((3, ta, width), BF),
-            pltpu.VMEM((2, tb, ff), BF),
-            pltpu.VMEM((2, tc, 3 * width), BF),
+            pltpu.VMEM((4, ta, width), BF),
+            pltpu.VMEM((3, tb, ff), BF),
+            pltpu.VMEM((3, tc, 3 * width), BF),
+            pltpu.SemaphoreType.DMA((4,)),
             pltpu.SemaphoreType.DMA((3,)),
-            pltpu.SemaphoreType.DMA((2,)),
-            pltpu.SemaphoreType.DMA((2,)),
+            pltpu.SemaphoreType.DMA((3,)),
             pltpu.SemaphoreType.DMA((2, 7)),
             pltpu.SemaphoreType.DMA((1,)),
         ]

time: 291 us -> 285 us (0.979)
  Pallas kernels: 280 us -> 273 us
    pallas_call x1, Pallas kernels: 77.3 us -> 70.8 us  [backward(): pl.pallas_call(functools.partial(backward_kernel, layers, sizes), out_sha...]
where the time goes in v4:
time: 285 us; the launch traced here: 284 us
  Pallas kernels  273 us (96%)
  other arithmetic  7.82 us (3%)
    pallas_call x1, Pallas kernels, forward(): pl.pallas_call(functools.partial(forward_kernel, layers, sizes), out_shap...  203 us
    pallas_call x1, Pallas kernels, backward(): pl.pallas_call(functools.partial(backward_kernel, layers, sizes), out_sha...  70.8 us
    concatenate x2, other arithmetic, turned_by(): jnp.concatenate([a, a], axis=0)  6.98 us

profile of v4, /device:TPU:0, one launch (start us, length us, event | category | flops | bytes accessed | tf_op | source)
XLA Modules:
  0.0 284.4 jit_solution(7620626941765117574)
XLA Ops:
  0.6 202.6 %forward.1 = (bf16[512,1024]{1,0:T(8,128)(2,1)}, f32[8,1024]{1,0:T(8,128)}, s32[1]{0:T(128)}, bf16[512,1024]{1,0:T(8,128)(2,1)}, bf16[2,3,512,1024]{3,2,1,0:T(8,...) custom-call(s32[1,2]{1,0:T(1,128)} %refs_0_.1, ...), custom_call_target="tpu_custom_call" | custom-call | tf_op jit(solution)/shard_map/forward/pallas_call | solution.py:867
  203.8 3.2 %fusion.1 = bf16[512,1024]{1,0:T(8,128)(2,1)} fusion(u32[]{:T(128)} %bitcast, bf16[512,1024]{1,0:T(8,128)(2,1)} %get-tuple-element.25), kind=kLoop, calls=%fused_computation.5 | loop fusion | flops 2097152 | bytes 2097156 | tf_op jit(solution)/shard_map/concatenate | solution.py:913
  207.0 70.8 %backward.1 = (f32[512,1024]{1,0:T(8,128)}, f32[2,16,1024]{2,1,0:T(8,128)}) custom-call(bf16[512,1024]{1,0:T(8,128)(2,1)} %get-tuple-element.27.refs_0_, f32[2,2,1024]{2,1,0:T(2,128)} %refs_1_.3, f32[8,1024]{1,0:T(8,128)} %get-tuple-element.28.refs_2_, bf16[2,3,512,1024]{3,2,1,0:T(8,128)(2,1)} %get-tuple-element.29.refs_3_, ...), custom_call_target="tpu_custom_call" | custom-call | tf_op jit(solution)/shard_map/backward/pallas_call | solution.py:407
  277.8 0.0 copy-start
  277.8 3.8 %fusion = f32[512,1024]{1,0:T(8,128)} fusion(u32[]{:T(128)} %bitcast, f32[512,1024]{1,0:T(8,128)} %get-tuple-element.40), kind=kLoop, calls=%fused_computation.2 | loop fusion | flops 524288 | bytes 4194308 | tf_op jit(solution)/shard_map/concatenate | solution.py:913
  281.6 0.0 copy-done
  281.6 0.1 multiply_reduce_fusion
  281.7 0.1 slice_reduce_fusion
  281.8 0.6 divide_sqrt_fusion
  282.5 0.6 copy_bitcast_fusion
  283.1 0.6 fusion.3
  283.7 0.6 copy.23
  (2 shorter events, 0.0 us)
Async XLA Ops:
  277.8 3.8 %copy-start = (f32[2,16,1024]{2,1,0:T(8,128)S(1)}, f32[2,16,1024]{2,1,0:T(8,128)}, u32[]{:S(2)}) copy-start(f32[2,16,1024]{2,1,0:T(8,128)} %get-tuple-element.41) | copy-start | bytes 393220

commit v5 on v4

--- a/solution.py
+++ b/solution.py
@@ -223,7 +223,7 @@
     ra.prime()
     load(1, order[0], 0).start()
 
-    chunk = 32
+    chunk = 64
     cot_copy.wait()
 
     def widen(c, carry):
@@ -605,7 +605,7 @@
     def free(src, dst, key, when):
         pl.when(when)(lambda: pltpu.make_async_copy(src, dst, sem_save.at[key]).wait())
 
-    chunk = 32
+    chunk = 64
     steps = slots // chunk
 
     def rows_of(c):

time: 285 us -> 279 us (0.979)
  Pallas kernels: 273 us -> 268 us
    pallas_call x1, Pallas kernels: 70.8 us -> 67.6 us  [backward(): pl.pallas_call(functools.partial(backward_kernel, layers, sizes), out_sha...]
where the time goes in v5:
time: 279 us
  Pallas kernels  268 us (96%)
  other arithmetic  7.82 us (3%)
    pallas_call x1, Pallas kernels, forward(): pl.pallas_call(functools.partial(forward_kernel, layers, sizes), out_shap...  200 us
    pallas_call x1, Pallas kernels, backward(): pl.pallas_call(functools.partial(backward_kernel, layers, sizes), out_sha...  67.6 us
    concatenate x2, other arithmetic, turned_by(): jnp.concatenate([a, a], axis=0)  6.98 us

profile of v5, /device:TPU:0, one launch (start us, length us, event | category | flops | bytes accessed | tf_op | source)
XLA Modules:
  0.0 279.0 jit_solution(7825404785740411182)
XLA Ops:
  0.6 200.4 %forward.1 = (bf16[512,1024]{1,0:T(8,128)(2,1)}, f32[8,1024]{1,0:T(8,128)}, s32[1]{0:T(128)}, bf16[512,1024]{1,0:T(8,128)(2,1)}, bf16[2,3,512,1024]{3,2,1,0:T(8,...) custom-call(s32[1,2]{1,0:T(1,128)} %refs_0_.1, ...), custom_call_target="tpu_custom_call" | custom-call | tf_op jit(solution)/shard_map/forward/pallas_call | solution.py:867
  201.7 3.2 %fusion.1 = bf16[512,1024]{1,0:T(8,128)(2,1)} fusion(u32[]{:T(128)} %bitcast, bf16[512,1024]{1,0:T(8,128)(2,1)} %get-tuple-element.25), kind=kLoop, calls=%fused_computation.5 | loop fusion | flops 2097152 | bytes 2097156 | tf_op jit(solution)/shard_map/concatenate | solution.py:913
  204.9 67.6 %backward.1 = (f32[512,1024]{1,0:T(8,128)}, f32[2,16,1024]{2,1,0:T(8,128)}) custom-call(bf16[512,1024]{1,0:T(8,128)(2,1)} %get-tuple-element.27.refs_0_, f32[2,2,1024]{2,1,0:T(2,128)} %refs_1_.3, f32[8,1024]{1,0:T(8,128)} %get-tuple-element.28.refs_2_, bf16[2,3,512,1024]{3,2,1,0:T(8,128)(2,1)} %get-tuple-element.29.refs_3_, ...), custom_call_target="tpu_custom_call" | custom-call | tf_op jit(solution)/shard_map/backward/pallas_call | solution.py:407
  272.4 0.0 copy-start
  272.5 3.8 %fusion = f32[512,1024]{1,0:T(8,128)} fusion(u32[]{:T(128)} %bitcast, f32[512,1024]{1,0:T(8,128)} %get-tuple-element.40), kind=kLoop, calls=%fused_computation.2 | loop fusion | flops 524288 | bytes 4194308 | tf_op jit(solution)/shard_map/concatenate | solution.py:913
  276.2 0.0 copy-done
  276.3 0.1 multiply_reduce_fusion
  276.4 0.1 slice_reduce_fusion
  276.5 0.6 divide_sqrt_fusion
  277.1 0.6 copy_bitcast_fusion
  277.7 0.6 fusion.3
  278.4 0.6 copy.23
  (2 shorter events, 0.0 us)
Async XLA Ops:
  272.4 3.8 %copy-start = (f32[2,16,1024]{2,1,0:T(8,128)S(1)}, f32[2,16,1024]{2,1,0:T(8,128)}, u32[]{:S(2)}) copy-start(f32[2,16,1024]{2,1,0:T(8,128)} %get-tuple-element.41) | copy-start | bytes 393220
